TPU v7x, 32 devices: a whole 2x2x4 slice. The times are simulated.
32 devices in a mesh: users: 2 (over x), ctx: 4 (over z), head: 4 (over y, core).
Axes of the slice: x: 2, y: 2, z: 4, core: 2. Of those that a mesh axis runs over, the one named last changes fastest.
Arguments:
- counts: int32 [2], P('users'), may hold values from 64 to 512, as said below
- cand_owner: int32 [2, 512, 1], P('users', 'ctx'), may hold values from 0 to 7; in each aligned block of 128 rows (0 to 127, 128 to 255, ..., all dimensions but the last counted through in order) at most 32 rows name the same one
- cand_row: int32 [2, 512], P('users', 'ctx'), may hold values from 0 to 127
- item_table: bfloat16 [1024, 1024], P(('users', 'ctx')), may hold values from -6 to 6
- proj_weight: bfloat16 [1024, 4, 1024], P(None, None, 'head'), may hold values from -0.1875 to 0.1875
- out_weight: bfloat16 [1024, 1024], P('head'), may hold values from -0.1875 to 0.1875
- key_cache: bfloat16 [2, 2048, 1024], P('users', 'ctx', 'head'), may hold values from -6 to 6
- value_cache: bfloat16 [2, 2048, 1024], P('users', 'ctx', 'head'), may hold values from -6 to 6
Outputs:
- mixed: bfloat16 [2, 512, 1024], P('users', 'ctx', 'head')
Inputs may be any that keep to these rules, and one draw needn't show every extreme that they name: `counts`: some user has all 512 slots live. `cand_owner`: among the 128 slots of one user on one index of ctx, at most 32 name the same owner, a bound that some block reaches.
All inputs are finite; a program needn't handle non-finite values.
Results may differ from a plain program's by a relative error of at most 0.0056.
Values may be sent and summed in bfloat16 or wider, within the bound.
No kernel may reach another device: no remote copies, remote signals or barrier semaphores. Data moves between devices by JAX's collectives and lax.ppermute only.
A program may use at most 64 MiB of HBM per device.

v0:
```python
import jax
import jax.numpy as jnp
from jax import lax
from jax.experimental import pallas as pl
from jax.experimental.pallas import tpu as pltpu
from jax.sharding import PartitionSpec as P


HEAD_DIM = 128
PAD = 16
F32 = jnp.float32
BF16 = jnp.bfloat16


def silu(v):
    return 0.5 * v * (1.0 + jnp.tanh(0.5 * v))


def dot(a, b):
    return jnp.dot(a, b, preferred_element_type=F32)


def vmem():
    return pl.BlockSpec(memory_space=pltpu.VMEM)


def call(kernel, outs, scratch=(), specs=None):
    given = {} if specs is None else {"in_specs": specs}
    return pl.pallas_call(
        kernel, out_shape=outs, out_specs=jax.tree.map(lambda _: vmem(), outs), scratch_shapes=list(scratch), **given
    )


def shape(dims, kind=BF16):
    return jax.ShapeDtypeStruct(dims, kind)


def normed_of(table_ref):
    x = table_ref[...].astype(F32)
    center = x - jnp.mean(x, axis=1, keepdims=True)
    return (center * lax.rsqrt(jnp.mean(center * center, axis=1, keepdims=True) + 1e-05)).astype(BF16)


def project_kernel(owner_ref, row_ref, table_ref, weight_hbm, packet_ref, bulk_ref, weight_ref, sems):
    rows, model = table_ref.shape
    kinds, width = weight_ref.shape[1:]
    slots = owner_ref.shape[1]
    step = model // sems.shape[0]
    lanes = 128 * kinds
    copies = [
        pltpu.make_async_copy(weight_hbm.at[at : at + step], weight_ref.at[at : at + step], sems.at[at // step])
        for at in range(0, model, step)
    ]
    for one in copies:
        one.start()
    packet_ref[rows:, 0:slots] = jnp.broadcast_to(owner_ref[...].astype(F32), (PAD, slots)).astype(BF16)
    packet_ref[rows:, slots : 2 * slots] = jnp.broadcast_to(row_ref[...].astype(F32), (PAD, slots)).astype(BF16)
    start = pl.multiple_of(lax.axis_index("head") * width, width)
    bulk_ref[2 * rows : 3 * rows, :] = table_ref[:, pl.ds(start, width)]
    normed = normed_of(table_ref)
    spread = (
        lax.broadcasted_iota(jnp.int32, (128, lanes), 1) // kinds
        == lax.broadcasted_iota(jnp.int32, (128, lanes), 0)
    ).astype(F32).astype(BF16)
    kind = lax.broadcasted_iota(jnp.int32, (rows, lanes), 1) % kinds
    masks = [(kind == k).astype(F32).astype(BF16) for k in range(kinds)]
    total = jnp.zeros((kinds * rows, width), F32)
    for at in range(0, model, 128):
        wide = dot(normed[:, at : at + 128], spread).astype(BF16)
        left = jnp.concatenate([wide * mask for mask in masks], axis=0)
        if at % step == 0:
            copies[at // step].wait()
        total = total + dot(left, weight_ref[at : at + 128].reshape(lanes, width))
    gates, values, queries, keys = [silu(total[k * rows : (k + 1) * rows]).astype(BF16) for k in range(kinds)]
    packet_ref[0:rows, :] = queries
    bulk_ref[rows : 2 * rows, :] = gates
    bulk_ref[3 * rows :, :] = queries
    product = queries.astype(F32) * keys.astype(F32)
    for first in range(0, width, HEAD_DIM):
        cols = slice(first, first + HEAD_DIM)
        score = jnp.sum(product[:, cols], axis=1, keepdims=True)
        bulk_ref[0:rows, cols] = (silu(score * HEAD_DIM ** (-0.5)) * values[:, cols].astype(F32)).astype(BF16)


def one_hot(spot, size):
    lanes = lax.broadcasted_iota(jnp.int32, (spot.shape[0], size), 1).astype(F32)
    return (lanes == spot).astype(F32).astype(BF16)


def loop(size, body):
    if size <= 4:
        for j in range(size):
            body(j)
    else:
        lax.fori_loop(0, size, lambda j, c: (body(j), c)[1], 0)


def sort_kernel(users, ctx_size, held, *refs):
    packets = refs[:ctx_size]
    bulks = refs[ctx_size : ctx_size + users]
    outs = refs[ctx_size + users :]
    sends = outs[: ctx_size - 1]
    mine_ref, own_ref, query_ref, spot_ref, id_ref = outs[ctx_size - 1 :]
    me_user = lax.axis_index("users")
    me_ctx = lax.axis_index("ctx")
    rows = bulks[0].shape[0] // 4
    width = bulks[0].shape[1]
    slots = mine_ref.shape[0]
    owners = [
        [((me_user ^ k) * ctx_size + (me_ctx ^ m)).astype(F32) for m in range(ctx_size)] for k in range(users)
    ]
    for m in range(ctx_size):
        id_ref[m] = jnp.transpose(packets[m][rows:, :].astype(F32))
    lane = lax.broadcasted_iota(jnp.int32, (slots, 128), 1)

    def place(j):
        owner = id_ref[j, 0:slots, 0:1]
        row = id_ref[j, slots : 2 * slots, 0:1]
        spots = jnp.full((slots, 128), -1.0, F32)
        group = jnp.full((slots, 1), -1.0, F32)
        for k in range(users):
            spot = jnp.full((slots, 1), -1.0, F32)
            for m in range(ctx_size):
                spot = jnp.where(owner == owners[k][m], row + float(m * rows), spot)
            spots = jnp.where(lane == k, spot, spots)
            group = jnp.where(owner == owners[k][0], row + float(k * rows), group)
        first = j * slots if isinstance(j, int) else pl.multiple_of(j * slots, slots)
        spot_ref[pl.ds(first, slots), :] = spots
        pick = one_hot(spots[:, 0:1], ctx_size * rows)
        total = jnp.zeros((slots, width), F32)
        for m in range(ctx_size):
            total = total + dot(pick[:, m * rows : (m + 1) * rows], packets[m][0:rows, :])
        query_ref[pl.ds(first, slots), :] = total.astype(BF16)
        pick = one_hot(group, users * rows)
        own = jnp.zeros((slots, width), F32)
        for k in range(users):
            own = own + dot(pick[:, k * rows : (k + 1) * rows], bulks[k][0:rows, :])
        own_ref[pl.ds(first, slots), :] = own.astype(BF16)

    loop(ctx_size, place)
    before = (
        lax.broadcasted_iota(jnp.int32, (slots, slots), 0) < lax.broadcasted_iota(jnp.int32, (slots, slots), 1)
    ).astype(F32).astype(BF16)
    for j in range(ctx_size):
        owner = id_ref[j, 0:slots, 0:1]
        row = id_ref[j, slots : 2 * slots, 0:1]
        group = jnp.full((slots, 1), -1.0, F32)
        for k in range(users):
            group = jnp.where(owner == owners[k][0], row + float(k * rows), group)
        pick = one_hot(group, users * rows)
        if j > 0:
            line = packets[j][rows:, 0:slots].astype(F32)
            inside = jnp.zeros(line.shape, jnp.bool_)
            for k in range(users):
                inside = inside | (line == owners[k][0])
            rank = jnp.where(inside, dot(inside.astype(F32).astype(BF16), before), -1.0)[0:1, :]
            keep = lax.broadcasted_iota(jnp.int32, (held, slots), 0).astype(F32) == rank
            pick = dot(keep.astype(F32).astype(BF16), pick).astype(BF16)
        for part in range(2):
            total = jnp.zeros((pick.shape[0], width), F32)
            for k in range(users):
                total = total + dot(
                    pick[:, k * rows : (k + 1) * rows], bulks[k][(part + 1) * rows : (part + 2) * rows, :]
                )
            if j > 0:
                sends[j - 1][part * held : (part + 1) * held, :] = total.astype(BF16)
            else:
                mine_ref[:, part * width : (part + 1) * width] = total.astype(BF16)


def attend_kernel(users, ctx_size, rows, history, places, *refs):
    spot_ref, part_ref, own_ref, key_ref, value_ref = refs[:5]
    packs = refs[5 : 4 + ctx_size]
    outs = refs[-ctx_size - 2 : -2]
    others = refs[4 + ctx_size : -ctx_size - 2]
    query_ref, sum_ref = refs[-2:]
    width = key_ref.shape[1]
    slots = outs[0].shape[0]

    def place(j):
        first = j * slots if isinstance(j, int) else pl.multiple_of(j * slots, slots)
        total = part_ref[pl.ds(first, slots), :].astype(F32)
        for k in range(1, users):
            pick = one_hot(spot_ref[pl.ds(first, slots), k : k + 1], ctx_size * rows)
            for m in range(ctx_size):
                which, at = places[k, m]
                total = total + dot(pick[:, m * rows : (m + 1) * rows], others[which][at : at + rows, :])
        query_ref[pl.ds(first, slots), :] = total.astype(BF16)

    loop(ctx_size, place)
    count = ctx_size * slots
    block = min(count, 512)

    def attend(b):
        first = b * block if isinstance(b, int) else pl.multiple_of(b * block, block)
        for at in range(0, width, HEAD_DIM):
            cols = slice(at, at + HEAD_DIM)
            scores = lax.dot_general(
                query_ref[pl.ds(first, block), cols], key_ref[:, cols],
                (((1,), (1,)), ((), ())), preferred_element_type=F32,
            ) * (0.5 * HEAD_DIM ** (-0.5))
            weights = (scores + scores * jnp.tanh(scores)).astype(BF16)
            sum_ref[pl.ds(first, block), cols] = dot(weights, value_ref[:, cols])

    loop(count // block, attend)
    for j in range(ctx_size):
        span = slice(j * slots, (j + 1) * slots)
        outs[j][0:slots, :] = (sum_ref[span, :] * history ** (-0.5) + own_ref[span, :].astype(F32)).astype(BF16)
        if j > 0:
            outs[j][slots:, :] = packs[j - 1][...]


def mix_kernel(users, ctx_size, head_size, held, *refs):
    owner_ref, mine_ref, weight_ref = refs[:3]
    sums = refs[3 : 3 + ctx_size]
    outs = refs[3 + ctx_size : 3 + ctx_size + head_size]
    residual_ref = refs[3 + ctx_size + head_size]
    me_user = lax.axis_index("users")
    me_ctx = lax.axis_index("ctx")
    me_head = lax.axis_index("head")
    slots, width = mine_ref.shape[0], mine_ref.shape[1] // 2
    owner = jnp.transpose(jnp.broadcast_to(owner_ref[...].astype(F32), (8, slots)))[:, 0:1]
    lanes = 128
    lane = lax.broadcasted_iota(jnp.int32, (slots, lanes), 1)
    inside = jnp.zeros((slots, lanes), jnp.bool_)
    for k in range(users):
        named = (me_user ^ k) * ctx_size + (me_ctx ^ lane)
        inside = inside | ((owner == named.astype(F32)) & (lane < ctx_size))
    after = (
        lax.broadcasted_iota(jnp.int32, (slots, slots), 1) < lax.broadcasted_iota(jnp.int32, (slots, slots), 0)
    ).astype(F32).astype(BF16)
    rank = jnp.where(inside, dot(after, inside.astype(F32).astype(BF16)), -1.0)
    attended = sums[0][...].astype(F32)
    gates = mine_ref[:, 0:width].astype(F32)
    residual = mine_ref[:, width:].astype(F32)
    spots = lax.broadcasted_iota(jnp.int32, (slots, held), 1).astype(F32)
    for m in range(1, ctx_size):
        attended = attended + sums[m][0:slots, :].astype(F32)
        pick = (spots == rank[:, m : m + 1]).astype(F32).astype(BF16)
        gates = gates + dot(pick, sums[m][slots : slots + held, :])
        residual = residual + dot(pick, sums[m][slots + held :, :])
    residual_ref[...] = residual.astype(BF16)
    parts = []
    for at in range(0, width, HEAD_DIM):
        one = attended[:, at : at + HEAD_DIM]
        center = one - jnp.mean(one, axis=1, keepdims=True)
        parts.append(
            center
            * lax.rsqrt(jnp.mean(center * center, axis=1, keepdims=True) + 1e-05)
            * gates[:, at : at + HEAD_DIM]
        )
    hidden = jnp.concatenate(parts, axis=1).astype(BF16)
    for t in range(head_size):
        first = pl.multiple_of((me_head ^ t) * width, width)
        outs[t][...] = dot(hidden, weight_ref[:, pl.ds(first, width)]).astype(outs[t].dtype)


def swap(x, axis, k):
    return lax.ppermute(x, axis, [(i, i ^ k) for i in range(lax.axis_size(axis))])


def layer(
    counts, cand_owner, cand_row, item_table, proj_weight, out_weight, key_cache, value_cache
):
    users = lax.axis_size("users")
    ctx_size = lax.axis_size("ctx")
    head_size = lax.axis_size("head")
    slots = cand_row.shape[1]
    rows, model = item_table.shape
    width = proj_weight.shape[2]
    span = rows + PAD
    history = key_cache.shape[1] * ctx_size
    capacity = max(2, 2 * slots // (users * ctx_size))
    held = max(PAD, -(-users * min(capacity, slots) // PAD) * PAD)
    owner = cand_owner.reshape(1, slots)
    kinds = proj_weight.shape[1]
    stage = (pltpu.VMEM((model, kinds, width), BF16), pltpu.SemaphoreType.DMA((4,)))
    hbm = pl.BlockSpec(memory_space=pl.ANY)
    packet, bulk = call(
        project_kernel, (shape((span, width)), shape((4 * rows, width))), stage, specs=[vmem()] * 3 + [hbm]
    )(owner, cand_row, item_table, proj_weight)
    packets = [packet] + [swap(packet, "ctx", m) for m in range(1, ctx_size)]
    bulks = [bulk] + [swap(bulk, "users", k) for k in range(1, users)]
    relays, places = [], {}
    for k in range(1, users):
        places[k, 0] = (len(relays), 3 * rows)
        relays.append(bulks[k])
    if users * ctx_size <= 8:
        for m in range(1, ctx_size):
            for k in range(1, users):
                places[k, m] = (len(relays), 0)
                relays.append(swap(packets[m], "users", k))
    elif ctx_size > 1:
        joined = jnp.concatenate(packets[1:], axis=0)
        for k in range(1, users):
            for m in range(1, ctx_size):
                places[k, m] = (len(relays), (m - 1) * span)
            relays.append(swap(joined, "users", k))
    count = ctx_size * slots
    *packs, mine, own, part, spots = call(
        lambda *refs: sort_kernel(users, ctx_size, held, *refs),
        (shape((2 * held, width)),) * (ctx_size - 1)
        + (shape((slots, 2 * width)), shape((count, width)), shape((count, width)), shape((count, 128), F32)),
        (pltpu.VMEM((ctx_size, width, PAD), F32),),
    )(*packets, *bulks)
    sums = call(
        lambda *refs: attend_kernel(users, ctx_size, rows, history, places, *refs),
        (shape((slots, width)),) + (shape((slots + 2 * held, width)),) * (ctx_size - 1),
        (pltpu.VMEM((count, width), BF16), pltpu.VMEM((count, width), F32)),
    )(spots, part, own, key_cache[0], value_cache[0], *packs, *relays)
    sums = [sums[0]] + [swap(sums[m], "ctx", m) for m in range(1, ctx_size)]
    *parts, residual = call(
        lambda *refs: mix_kernel(users, ctx_size, head_size, held, *refs),
        (shape((slots, width), F32),) + (shape((slots, width)),) * (head_size - 1) + (shape((slots, width)),),
    )(owner, mine, out_weight, *sums)
    got = [parts[0]] + [swap(parts[t], "head", t) for t in range(1, head_size)]
    total = residual.astype(F32)
    for one in got:
        total = total + one.astype(F32)
    slot = lax.axis_index("ctx") * slots + jnp.arange(slots, dtype=jnp.int32)
    return jnp.where((slot < counts[0])[:, None], total, 0.0).astype(BF16)[None]


def solution(mesh):
    return jax.shard_map(
        layer,
        mesh=mesh,
        in_specs=(
            P("users"),
            P("users", "ctx", None),
            P("users", "ctx"),
            P(("users", "ctx"), None),
            P(None, None, "head"),
            P("head", None),
            P("users", "ctx", "head"),
            P("users", "ctx", "head"),
        ),
        out_specs=P("users", "ctx", "head"),
        check_vma=False,
    )
```

profile of v0, /device:TPU:0, one launch (start us, length us, event | category | flops | bytes accessed | tf_op | source)
XLA Modules:
  0.0 52.4 jit_solution(6437289508039309436)
XLA Ops:
  0.0 5.7 %shard_map.82 = (bf16[144,256]{1,0:T(8,128)(2,1)}, bf16[512,256]{1,0:T(8,128)(2,1)}) custom-call(s32[1,128]{1,0:T(1,128)} %bitcast.9, s32[1,128]{1,0:T(1,128)} %row_ref.1, bf16[128,1024]{1,0:T(8,128)(2,1)} %table_ref.1, bf16[1024,4,256]{2,1,0:T(4,128)(2,1)} %weight_hbm.1), custom_call_target="tpu_custom_call" | custom-call | tf_op jit(solution)/shard_map/pallas_call | solution.py:279
  5.7 3.0 %collective-permute-start.3 = (bf16[512,256]{1,0:T(8,128)(2,1)}, bf16[512,256]{1,0:T(8,128)(2,1)S(1)}, u32[]{:S(2)}, u32[]{:S(2)}) collective-permute-start(bf16[512,256]{1,0:T(8,128)(2,1)} %get-tuple-element.24.refs_4_), channel_id=1, source_target_pairs={{0,16},{16,0},{1,17},{17,1},{2,18},{18,2},{3,19},{19,3},{4,20},{20... | collective-permute-start | bytes 786440 | tf_op jit(solution)/shard_map/ppermute | solution.py:259
  8.8 1.6 %collective-permute-start = (bf16[144,256]{1,0:T(8,128)(2,1)}, bf16[144,256]{1,0:T(8,128)(2,1)S(1)}, u32[]{:S(2)}, u32[]{:S(2)}) collective-permute-start(bf16[144,256]{1,0:T(8,128)(2,1)} %get-tuple-element.23.refs_0_), channel_id=1, source_target_pairs={{0,4},{4,0},{8,12},{12,8},{1,5},{5,1},{9,13},{13,9},{2,6},{6,2},{1... | collective-permute-start | bytes 221192 | tf_op jit(solution)/shard_map/ppermute | solution.py:259
  10.3 2.6 %collective-permute-start.1 = (bf16[144,256]{1,0:T(8,128)(2,1)}, bf16[144,256]{1,0:T(8,128)(2,1)S(1)}, u32[]{:S(2)}, u32[]{:S(2)}) collective-permute-start(bf16[144,256]{1,0:T(8,128)(2,1)} %get-tuple-element.23.refs_0_), channel_id=1, source_target_pairs={{0,8},{4,12},{8,0},{12,4},{1,9},{5,13},{9,1},{13,5},{2,10},{6,14},... | collective-permute-start | bytes 221192 | tf_op jit(solution)/shard_map/ppermute | solution.py:259
  12.9 0.2 collective-permute-start.2
  13.1 0.2 collective-permute-done.refs_1_
  13.3 0.0 copy-start.5
  13.3 0.2 collective-permute-start.4
  13.5 4.5 %collective-permute-done.1.refs_2_ = bf16[144,256]{1,0:T(8,128)(2,1)S(1)} collective-permute-done((bf16[144,256]{1,0:T(8,128)(2,1)}, bf16[144,256]{1,0:T(8,128)(2,1)S(1)}, u32[]{:S(2)}, u32[]{:S(2)}) %collective-permute-start.1) | collective-permute-done | bytes 73760 | tf_op jit(solution)/shard_map/ppermute | solution.py:259
  18.1 0.0 copy-start.6
  18.1 0.5 %collective-permute-start.5 = (bf16[144,256]{1,0:T(8,128)(2,1)S(1)}, bf16[144,256]{1,0:T(8,128)(2,1)S(1)}, u32[]{:S(2)}, u32[]{:S(2)}) collective-permute-start(bf16[144,256]{1,0:T(8,128)(2,1)S(1)} %collective-permute-done.1.refs_2_), channel_id=1, source_target_pairs={{0,16},{16,0},{1,17},{17,1},{2,18},{18,2},{3,19},{19,3},{4,20},{20... | collective-permute-start | bytes 221192 | tf_op jit(solution)/shard_map/ppermute | solution.py:259
  18.6 0.8 %collective-permute-done.2.refs_3_ = bf16[144,256]{1,0:T(8,128)(2,1)S(1)} collective-permute-done((bf16[144,256]{1,0:T(8,128)(2,1)}, bf16[144,256]{1,0:T(8,128)(2,1)S(1)}, u32[]{:S(2)}, u32[]{:S(2)}) %collective-permute-start.2) | collective-permute-done | bytes 73760 | tf_op jit(solution)/shard_map/ppermute | solution.py:259
  19.4 0.0 copy-start.7
  19.4 0.7 %collective-permute-start.6 = (bf16[144,256]{1,0:T(8,128)(2,1)S(1)}, bf16[144,256]{1,0:T(8,128)(2,1)S(1)}, u32[]{:S(2)}, u32[]{:S(2)}) collective-permute-start(bf16[144,256]{1,0:T(8,128)(2,1)S(1)} %collective-permute-done.2.refs_3_), channel_id=1, source_target_pairs={{0,16},{16,0},{1,17},{17,1},{2,18},{18,2},{3,19},{19,3},{4,20},{20... | collective-permute-start | bytes 221192 | tf_op jit(solution)/shard_map/ppermute | solution.py:259
  20.1 0.0 collective-permute-done.3.refs_5_.refs_8_
  20.1 0.0 copy-done.5
  20.1 0.0 copy-done.6
  20.1 0.0 copy-done.7
  20.1 0.0 copy-start
  20.1 0.7 %copy-done = bf16[512,256]{1,0:T(8,128)(2,1)} copy-done((bf16[512,256]{1,0:T(8,128)(2,1)}, bf16[512,256]{1,0:T(8,128)(2,1)S(1)}, u32[]{:S(2)}) %copy-start) | copy-done | bytes 262168
  20.8 3.7 %shard_map.83 = (bf16[128,256]{1,0:T(8,128)(2,1)}, bf16[128,256]{1,0:T(8,128)(2,1)}, bf16[128,256]{1,0:T(8,128)(2,1)}, bf16[128,512]{1,0:T(8,128)(2,1)}, bf16[51...) custom-call(bf16[144,256]{1,0:T(8,128)(2,1)} %get-tuple-element.23.refs_0_, ...), custom_call_target="tpu_custom_call" | custom-call | tf_op jit(solution)/shard_map/pallas_call | solution.py:300
  24.5 0.0 collective-permute-done.4.refs_9_
  24.5 0.0 copy-start.4
  24.5 0.0 collective-permute-done.5.refs_10_
  24.5 0.0 copy-start.8
  24.5 0.0 collective-permute-done.6.refs_11_
  24.5 0.0 copy-start.9
  24.6 0.6 %copy-done.4 = bf16[144,256]{1,0:T(8,128)(2,1)} copy-done((bf16[144,256]{1,0:T(8,128)(2,1)}, bf16[144,256]{1,0:T(8,128)(2,1)S(1)}, u32[]{:S(2)}) %copy-start.4) | copy-done | bytes 73752
  25.1 0.0 copy-done.8
  25.2 0.0 copy-done.9
  25.2 3.3 %shard_map.84 = (bf16[128,256]{1,0:T(8,128)(2,1)}, bf16[256,256]{1,0:T(8,128)(2,1)}, bf16[256,256]{1,0:T(8,128)(2,1)}, bf16[256,256]{1,0:T(8,128)(2,1)}) custom-call(f32[512,128]{1,0:T(8,128)} %get-tuple-element.26.refs_0_, bf16[512,256]{1,0:T(8,128)(2,1)} %get-tuple-element.27.refs_1_, bf16[512,256]{1,0:T(8,128)(2,1)} %get-tuple-element.28.refs_2_, ...), custom_call_target="tpu_custom_call" | custom-call | tf_op jit(solution)/shard_map/pallas_call | solution.py:306
  28.5 0.7 %collective-permute-start.7 = (bf16[256,256]{1,0:T(8,128)(2,1)}, bf16[256,256]{1,0:T(8,128)(2,1)S(1)}, u32[]{:S(2)}, u32[]{:S(2)}) collective-permute-start(bf16[256,256]{1,0:T(8,128)(2,1)} %get-tuple-element.33), channel_id=1, source_target_pairs={{0,4},{4,0},{8,12},{12,8},{1,5},{5,1},{9,13},{13,9},{2,6},{6,2},{1... | collective-permute-start | bytes 393224 | tf_op jit(solution)/shard_map/ppermute | solution.py:259
  29.3 3.1 %collective-permute-start.8 = (bf16[256,256]{1,0:T(8,128)(2,1)}, bf16[256,256]{1,0:T(8,128)(2,1)S(1)}, u32[]{:S(2)}, u32[]{:S(2)}) collective-permute-start(bf16[256,256]{1,0:T(8,128)(2,1)} %get-tuple-element.34), channel_id=1, source_target_pairs={{0,8},{4,12},{8,0},{12,4},{1,9},{5,13},{9,1},{13,5},{2,10},{6,14},... | collective-permute-start | bytes 393224 | tf_op jit(solution)/shard_map/ppermute | solution.py:259
  32.4 0.6 %collective-permute-start.9 = (bf16[256,256]{1,0:T(8,128)(2,1)}, bf16[256,256]{1,0:T(8,128)(2,1)S(1)}, u32[]{:S(2)}, u32[]{:S(2)}) collective-permute-start(bf16[256,256]{1,0:T(8,128)(2,1)} %get-tuple-element.35), channel_id=1, source_target_pairs={{0,12},{4,8},{8,4},{12,0},{1,13},{5,9},{9,5},{13,1},{2,14},{6,10},... | collective-permute-start | bytes 393224 | tf_op jit(solution)/shard_map/ppermute | solution.py:259
  33.6 0.3 collective-permute-done.7.refs_4_
  33.9 0.0 copy-start.1
  33.9 7.4 %collective-permute-done.8.refs_5_ = bf16[256,256]{1,0:T(8,128)(2,1)S(1)} collective-permute-done((bf16[256,256]{1,0:T(8,128)(2,1)}, bf16[256,256]{1,0:T(8,128)(2,1)S(1)}, u32[]{:S(2)}, u32[]{:S(2)}) %collective-permute-start.8) | collective-permute-done | bytes 131104 | tf_op jit(solution)/shard_map/ppermute | solution.py:259
  41.3 0.0 copy-start.2
  41.3 0.0 collective-permute-done.9.refs_6_
  41.3 0.0 copy-start.3
  41.3 0.0 copy-done.1
  41.3 0.6 %copy-done.2 = bf16[256,256]{1,0:T(8,128)(2,1)} copy-done((bf16[256,256]{1,0:T(8,128)(2,1)}, bf16[256,256]{1,0:T(8,128)(2,1)S(1)}, u32[]{:S(2)}) %copy-start.2) | copy-done | bytes 131096
  42.0 0.1 copy-done.3
  42.0 2.8 %shard_map.85 = (f32[128,256]{1,0:T(8,128)}, bf16[128,256]{1,0:T(8,128)(2,1)}, bf16[128,256]{1,0:T(8,128)(2,1)}, bf16[128,256]{1,0:T(8,128)(2,1)}, bf16[128,256]{1,0:T(8,128)(2,1)}) custom-call(s32[1,128]{1,0:T(1,128)} %bitcast.10, bf16[128,512]{1,0:T(8,128)(2,1)} %get-tuple-element.25.refs_1_, bf16[256,1024]{1,0:T(8,128)(2,1)} %refs_2_.1, ...), custom_call_target="tpu_custom_call" | custom-call | tf_op jit(solution)/shard_map/pallas_call | solution.py:312
  44.8 0.0 collective-permute-start.12
  44.8 1.5 %collective-permute-start.11 = (bf16[128,256]{1,0:T(8,128)(2,1)}, bf16[128,256]{1,0:T(8,128)(2,1)S(1)}, u32[]{:S(2)}, u32[]{:S(2)}) collective-permute-start(bf16[128,256]{1,0:T(8,128)(2,1)} %get-tuple-element.39), channel_id=1, source_target_pairs={{0,2},{1,3},{2,0},{3,1},{4,6},{5,7},{6,4},{7,5},{8,10},{9,11},{10,... | collective-permute-start | bytes 196616 | tf_op jit(solution)/shard_map/ppermute | solution.py:259
  46.3 0.3 collective-permute-start.10
  46.7 2.7 %collective-permute-done.12 = bf16[128,256]{1,0:T(8,128)(2,1)S(1)} collective-permute-done((bf16[128,256]{1,0:T(8,128)(2,1)}, bf16[128,256]{1,0:T(8,128)(2,1)S(1)}, u32[]{:S(2)}, u32[]{:S(2)}) %collective-permute-start.12) | collective-permute-done | bytes 65568 | tf_op jit(solution)/shard_map/ppermute | solution.py:259
  49.3 1.5 %collective-permute-done.11 = bf16[128,256]{1,0:T(8,128)(2,1)S(1)} collective-permute-done((bf16[128,256]{1,0:T(8,128)(2,1)}, bf16[128,256]{1,0:T(8,128)(2,1)S(1)}, u32[]{:S(2)}, u32[]{:S(2)}) %collective-permute-start.11) | collective-permute-done | bytes 65568 | tf_op jit(solution)/shard_map/ppermute | solution.py:259
  50.8 0.0 collective-permute-done.10
  50.8 1.6 %fusion = bf16[1,128,256]{2,1,0:T(8,128)(2,1)} fusion(bf16[128,256]{1,0:T(8,128)(2,1)S(1)} %collective-permute-done.12, bf16[128,256]{1,0:T(8,128)(2,1)S(1)} %collective-permute-done.11, bf16[128,256]{1,0:T(8,128)(2,1)S(1)} %collective-permute-done.10, f32[128,256]{1,0:T(8,128)} %get-tuple-element.37, bf16[128,256]{1,0:T(8,128)(2,1)} %get-tuple-element.36, ...), kind=kLoop, calls=%fused_computation.1 | loop fusion | flops 327680 | bytes 458880 | tf_op jit(solution)/shard_map/broadcast_in_dim | solution.py:321
  (1 shorter events, 0.0 us)
Async XLA Ops:
  5.7 14.4 %collective-permute-start.3 = (bf16[512,256]{1,0:T(8,128)(2,1)}, bf16[512,256]{1,0:T(8,128)(2,1)S(1)}, u32[]{:S(2)}, u32[]{:S(2)}) collective-permute-start(bf16[512,256]{1,0:T(8,128)(2,1)} %get-tuple-element.24.refs_4_), channel_id=1, source_target_pairs={{0,16},{16,0},{1,17},{17,1},{2,18},{18,2},{3,19},{19,3},{4,20},{20... | collective-permute-start | bytes 786440 | tf_op jit(solution)/shard_map/ppermute | solution.py:259
  8.8 4.6 %collective-permute-start = (bf16[144,256]{1,0:T(8,128)(2,1)}, bf16[144,256]{1,0:T(8,128)(2,1)S(1)}, u32[]{:S(2)}, u32[]{:S(2)}) collective-permute-start(bf16[144,256]{1,0:T(8,128)(2,1)} %get-tuple-element.23.refs_0_), channel_id=1, source_target_pairs={{0,4},{4,0},{8,12},{12,8},{1,5},{5,1},{9,13},{13,9},{2,6},{6,2},{1... | collective-permute-start | bytes 221192 | tf_op jit(solution)/shard_map/ppermute | solution.py:259
  10.3 7.7 %collective-permute-start.1 = (bf16[144,256]{1,0:T(8,128)(2,1)}, bf16[144,256]{1,0:T(8,128)(2,1)S(1)}, u32[]{:S(2)}, u32[]{:S(2)}) collective-permute-start(bf16[144,256]{1,0:T(8,128)(2,1)} %get-tuple-element.23.refs_0_), channel_id=1, source_target_pairs={{0,8},{4,12},{8,0},{12,4},{1,9},{5,13},{9,1},{13,5},{2,10},{6,14},... | collective-permute-start | bytes 221192 | tf_op jit(solution)/shard_map/ppermute | solution.py:259
  12.9 6.5 %collective-permute-start.2 = (bf16[144,256]{1,0:T(8,128)(2,1)}, bf16[144,256]{1,0:T(8,128)(2,1)S(1)}, u32[]{:S(2)}, u32[]{:S(2)}) collective-permute-start(bf16[144,256]{1,0:T(8,128)(2,1)} %get-tuple-element.23.refs_0_), channel_id=1, source_target_pairs={{0,12},{4,8},{8,4},{12,0},{1,13},{5,9},{9,5},{13,1},{2,14},{6,10},... | collective-permute-start | bytes 221192 | tf_op jit(solution)/shard_map/ppermute | solution.py:259
  13.3 6.8 %copy-start.5 = (bf16[144,256]{1,0:T(8,128)(2,1)}, bf16[144,256]{1,0:T(8,128)(2,1)S(1)}, u32[]{:S(2)}) copy-start(bf16[144,256]{1,0:T(8,128)(2,1)S(1)} %collective-permute-done.refs_1_) | copy-start | bytes 221188
  13.3 11.2 %collective-permute-start.4 = (bf16[144,256]{1,0:T(8,128)(2,1)S(1)}, bf16[144,256]{1,0:T(8,128)(2,1)S(1)}, u32[]{:S(2)}, u32[]{:S(2)}) collective-permute-start(bf16[144,256]{1,0:T(8,128)(2,1)S(1)} %collective-permute-done.refs_1_), channel_id=1, source_target_pairs={{0,16},{16,0},{1,17},{17,1},{2,18},{18,2},{3,19},{19,3},{4,20},{20... | collective-permute-start | bytes 221192 | tf_op jit(solution)/shard_map/ppermute | solution.py:259
  18.1 2.0 %copy-start.6 = (bf16[144,256]{1,0:T(8,128)(2,1)}, bf16[144,256]{1,0:T(8,128)(2,1)S(1)}, u32[]{:S(2)}) copy-start(bf16[144,256]{1,0:T(8,128)(2,1)S(1)} %collective-permute-done.1.refs_2_) | copy-start | bytes 221188
  18.1 6.4 %collective-permute-start.5 = (bf16[144,256]{1,0:T(8,128)(2,1)S(1)}, bf16[144,256]{1,0:T(8,128)(2,1)S(1)}, u32[]{:S(2)}, u32[]{:S(2)}) collective-permute-start(bf16[144,256]{1,0:T(8,128)(2,1)S(1)} %collective-permute-done.1.refs_2_), channel_id=1, source_target_pairs={{0,16},{16,0},{1,17},{17,1},{2,18},{18,2},{3,19},{19,3},{4,20},{20... | collective-permute-start | bytes 221192 | tf_op jit(solution)/shard_map/ppermute | solution.py:259
  19.4 0.7 %copy-start.7 = (bf16[144,256]{1,0:T(8,128)(2,1)}, bf16[144,256]{1,0:T(8,128)(2,1)S(1)}, u32[]{:S(2)}) copy-start(bf16[144,256]{1,0:T(8,128)(2,1)S(1)} %collective-permute-done.2.refs_3_) | copy-start | bytes 221188
  19.4 5.2 %collective-permute-start.6 = (bf16[144,256]{1,0:T(8,128)(2,1)S(1)}, bf16[144,256]{1,0:T(8,128)(2,1)S(1)}, u32[]{:S(2)}, u32[]{:S(2)}) collective-permute-start(bf16[144,256]{1,0:T(8,128)(2,1)S(1)} %collective-permute-done.2.refs_3_), channel_id=1, source_target_pairs={{0,16},{16,0},{1,17},{17,1},{2,18},{18,2},{3,19},{19,3},{4,20},{20... | collective-permute-start | bytes 221192 | tf_op jit(solution)/shard_map/ppermute | solution.py:259
  20.1 0.7 %copy-start = (bf16[512,256]{1,0:T(8,128)(2,1)}, bf16[512,256]{1,0:T(8,128)(2,1)S(1)}, u32[]{:S(2)}) copy-start(bf16[512,256]{1,0:T(8,128)(2,1)S(1)} %collective-permute-done.3.refs_5_.refs_8_) | copy-start | bytes 786436
  24.5 0.6 %copy-start.4 = (bf16[144,256]{1,0:T(8,128)(2,1)}, bf16[144,256]{1,0:T(8,128)(2,1)S(1)}, u32[]{:S(2)}) copy-start(bf16[144,256]{1,0:T(8,128)(2,1)S(1)} %collective-permute-done.4.refs_9_) | copy-start | bytes 221188
  24.5 0.6 %copy-start.8 = (bf16[144,256]{1,0:T(8,128)(2,1)}, bf16[144,256]{1,0:T(8,128)(2,1)S(1)}, u32[]{:S(2)}) copy-start(bf16[144,256]{1,0:T(8,128)(2,1)S(1)} %collective-permute-done.5.refs_10_) | copy-start | bytes 221188
  24.5 0.6 %copy-start.9 = (bf16[144,256]{1,0:T(8,128)(2,1)}, bf16[144,256]{1,0:T(8,128)(2,1)S(1)}, u32[]{:S(2)}) copy-start(bf16[144,256]{1,0:T(8,128)(2,1)S(1)} %collective-permute-done.6.refs_11_) | copy-start | bytes 221188
  28.5 5.4 %collective-permute-start.7 = (bf16[256,256]{1,0:T(8,128)(2,1)}, bf16[256,256]{1,0:T(8,128)(2,1)S(1)}, u32[]{:S(2)}, u32[]{:S(2)}) collective-permute-start(bf16[256,256]{1,0:T(8,128)(2,1)} %get-tuple-element.33), channel_id=1, source_target_pairs={{0,4},{4,0},{8,12},{12,8},{1,5},{5,1},{9,13},{13,9},{2,6},{6,2},{1... | collective-permute-start | bytes 393224 | tf_op jit(solution)/shard_map/ppermute | solution.py:259
  29.3 12.1 %collective-permute-start.8 = (bf16[256,256]{1,0:T(8,128)(2,1)}, bf16[256,256]{1,0:T(8,128)(2,1)S(1)}, u32[]{:S(2)}, u32[]{:S(2)}) collective-permute-start(bf16[256,256]{1,0:T(8,128)(2,1)} %get-tuple-element.34), channel_id=1, source_target_pairs={{0,8},{4,12},{8,0},{12,4},{1,9},{5,13},{9,1},{13,5},{2,10},{6,14},... | collective-permute-start | bytes 393224 | tf_op jit(solution)/shard_map/ppermute | solution.py:259
  32.4 9.0 %collective-permute-start.9 = (bf16[256,256]{1,0:T(8,128)(2,1)}, bf16[256,256]{1,0:T(8,128)(2,1)S(1)}, u32[]{:S(2)}, u32[]{:S(2)}) collective-permute-start(bf16[256,256]{1,0:T(8,128)(2,1)} %get-tuple-element.35), channel_id=1, source_target_pairs={{0,12},{4,8},{8,4},{12,0},{1,13},{5,9},{9,5},{13,1},{2,14},{6,10},... | collective-permute-start | bytes 393224 | tf_op jit(solution)/shard_map/ppermute | solution.py:259
  33.9 7.4 %copy-start.1 = (bf16[256,256]{1,0:T(8,128)(2,1)}, bf16[256,256]{1,0:T(8,128)(2,1)S(1)}, u32[]{:S(2)}) copy-start(bf16[256,256]{1,0:T(8,128)(2,1)S(1)} %collective-permute-done.7.refs_4_) | copy-start | bytes 393220
  41.3 0.6 %copy-start.2 = (bf16[256,256]{1,0:T(8,128)(2,1)}, bf16[256,256]{1,0:T(8,128)(2,1)S(1)}, u32[]{:S(2)}) copy-start(bf16[256,256]{1,0:T(8,128)(2,1)S(1)} %collective-permute-done.8.refs_5_) | copy-start | bytes 393220
  41.3 0.7 %copy-start.3 = (bf16[256,256]{1,0:T(8,128)(2,1)}, bf16[256,256]{1,0:T(8,128)(2,1)S(1)}, u32[]{:S(2)}) copy-start(bf16[256,256]{1,0:T(8,128)(2,1)S(1)} %collective-permute-done.9.refs_6_) | copy-start | bytes 393220
  44.8 4.5 %collective-permute-start.12 = (bf16[128,256]{1,0:T(8,128)(2,1)}, bf16[128,256]{1,0:T(8,128)(2,1)S(1)}, u32[]{:S(2)}, u32[]{:S(2)}) collective-permute-start(bf16[128,256]{1,0:T(8,128)(2,1)} %get-tuple-element.40), channel_id=1, source_target_pairs={{0,3},{1,2},{2,1},{3,0},{4,7},{5,6},{6,5},{7,4},{8,11},{9,10},{10,... | collective-permute-start | bytes 196616 | tf_op jit(solution)/shard_map/ppermute | solution.py:259
  44.8 6.0 %collective-permute-start.11 = (bf16[128,256]{1,0:T(8,128)(2,1)}, bf16[128,256]{1,0:T(8,128)(2,1)S(1)}, u32[]{:S(2)}, u32[]{:S(2)}) collective-permute-start(bf16[128,256]{1,0:T(8,128)(2,1)} %get-tuple-element.39), channel_id=1, source_target_pairs={{0,2},{1,3},{2,0},{3,1},{4,6},{5,7},{6,4},{7,5},{8,10},{9,11},{10,... | collective-permute-start | bytes 196616 | tf_op jit(solution)/shard_map/ppermute | solution.py:259
  46.3 4.5 %collective-permute-start.10 = (bf16[128,256]{1,0:T(8,128)(2,1)}, bf16[128,256]{1,0:T(8,128)(2,1)S(1)}, u32[]{:S(2)}, u32[]{:S(2)}) collective-permute-start(bf16[128,256]{1,0:T(8,128)(2,1)} %get-tuple-element.38), channel_id=1, source_target_pairs={{0,1},{1,0},{2,3},{3,2},{4,5},{5,4},{6,7},{7,6},{8,9},{9,8},{10,11... | collective-permute-start | bytes 196616 | tf_op jit(solution)/shard_map/ppermute | solution.py:259
where the time goes:
time: 52.7 us; the launch traced here: 52.4 us
  waiting for transfers between devices  17.4 us (33%)
  Pallas kernels  15.5 us (29%)
  starting transfers between devices  15.1 us (29%)
  local copies, waits for them, and re-layouts  2.04 us (4%)
  other arithmetic  1.63 us (3%)
  between operations  0.75 us (1%)
    ppermute x13, waiting for transfers between devices, swap(): lax.ppermute(x, axis, [(i, i ^ k) for i in range(lax.axis_size(axis))])  17.4 us
    ppermute x13, starting transfers between devices, swap(): lax.ppermute(x, axis, [(i, i ^ k) for i in range(lax.axis_size(axis))])  15.1 us
    pallas_call x1, Pallas kernels, layer(): call(project_kernel, (shape((span, width)), shape((4 * rows, width))), st...  5.72 us
    pallas_call x1, Pallas kernels, layer(): call(lambda *refs: sort_kernel(users, ctx_size, held, *refs), (shape((2 *...  3.67 us
    pallas_call x1, Pallas kernels, layer(): call(lambda *refs: attend_kernel(users, ctx_size, rows, history, places,...  3.34 us
    pallas_call x1, Pallas kernels, layer(): call(lambda *refs: mix_kernel(users, ctx_size, head_size, held, *refs), (...  2.75 us
    unnamed x20, local copies, waits for them, and re-layouts  2.04 us
    broadcast_in_dim x1, other arithmetic, layer(): return jnp.where((slot < counts[0])[:, None], total, 0.0).astype(BF16)[None]  1.63 us
  transfers between devices with their start and end apart: 13, of which 7 were waited for; matrix products, arithmetic and copies ran while one was open for 0% of the time, Pallas kernels for 7%

commit v1 on v0

--- a/solution.py
+++ b/solution.py
@@ -24,11 +24,23 @@
     return pl.BlockSpec(memory_space=pltpu.VMEM)
 
 
-def call(kernel, outs, scratch=(), specs=None):
+def call(kernel, outs, scratch=(), specs=None, far=()):
     given = {} if specs is None else {"in_specs": specs}
-    return pl.pallas_call(
-        kernel, out_shape=outs, out_specs=jax.tree.map(lambda _: vmem(), outs), scratch_shapes=list(scratch), **given
+    made = pl.pallas_call(
+        kernel,
+        out_shape=jax.tree.map(lambda o: pltpu.VMEM(o.shape, o.dtype), outs),
+        out_specs=jax.tree.map(lambda _: vmem(), outs),
+        scratch_shapes=list(scratch),
+        compiler_params=pltpu.CompilerParams(vmem_limit_bytes=16 << 20),
+        **given,
     )
+
+    def run(*args):
+        spaces = [pltpu.HBM if i in far else pltpu.VMEM for i in range(len(args))]
+        args = [pltpu.with_memory_space_constraint(x, space) for x, space in zip(args, spaces)]
+        return made(*args)
+
+    return run
 
 
 def shape(dims, kind=BF16):
@@ -277,7 +289,11 @@
     stage = (pltpu.VMEM((model, kinds, width), BF16), pltpu.SemaphoreType.DMA((4,)))
     hbm = pl.BlockSpec(memory_space=pl.ANY)
     packet, bulk = call(
-        project_kernel, (shape((span, width)), shape((4 * rows, width))), stage, specs=[vmem()] * 3 + [hbm]
+        project_kernel,
+        (shape((span, width)), shape((4 * rows, width))),
+        stage,
+        specs=[vmem()] * 3 + [hbm],
+        far=(0, 1, 2, 3),
     )(owner, cand_row, item_table, proj_weight)
     packets = [packet] + [swap(packet, "ctx", m) for m in range(1, ctx_size)]
     bulks = [bulk] + [swap(bulk, "users", k) for k in range(1, users)]
@@ -317,8 +333,8 @@
     total = residual.astype(F32)
     for one in got:
         total = total + one.astype(F32)
-    slot = lax.axis_index("ctx") * slots + jnp.arange(slots, dtype=jnp.int32)
-    return jnp.where((slot < counts[0])[:, None], total, 0.0).astype(BF16)[None]
+    slot = lax.broadcasted_iota(jnp.int32, total.shape, 0)
+    return jnp.where(slot < counts[0] - lax.axis_index("ctx") * slots, total, 0.0).astype(BF16)[None]
 
 
 def solution(mesh):

time: 52.7 us -> 43.3 us (0.82)
  Pallas kernels: 15.5 us -> 8.96 us
  local copies, waits for them, and re-layouts: 2.04 us -> 0.01 us
  other arithmetic: 1.63 us -> 0.72 us
    pallas_call x4, Pallas kernels: 15.5 us -> 8.96 us  [run(): return made(*args)]
    unnamed x20 -> x8, local copies, waits for them, and re-layouts: 2.04 us -> 0.01 us
    broadcast_in_dim x1, other arithmetic: 1.63 us -> 0.72 us  [layer(): jnp.where(slot < counts[0] - lax.axis_index('ctx') * slots, total, 0.0)]
  transfers between devices with their start and end apart: 13 -> 13, of which waited for: 7 -> 8; matrix products, arithmetic and copies ran while one was open for 0% -> 0% of each run, Pallas kernels for 7% -> 4%
where the time goes in v1:
time: 43.3 us; the launch traced here: 43.1 us
  waiting for transfers between devices  17.4 us (40%)
  starting transfers between devices  15.3 us (35%)
  Pallas kernels  8.96 us (21%)
  other arithmetic  0.72 us (2%)
  between operations  0.72 us (2%)
    ppermute x13, waiting for transfers between devices, swap(): lax.ppermute(x, axis, [(i, i ^ k) for i in range(lax.axis_size(axis))])  17.4 us
    ppermute x13, starting transfers between devices, swap(): lax.ppermute(x, axis, [(i, i ^ k) for i in range(lax.axis_size(axis))])  15.3 us
    pallas_call x4, Pallas kernels, run(): return made(*args)  8.96 us
  transfers between devices with their start and end apart: 13, of which 8 were waited for; matrix products, arithmetic and copies ran while one was open for 0% of the time, Pallas kernels for 4%

profile of v1, /device:TPU:0, one launch (start us, length us, event | category | flops | bytes accessed | tf_op | source)
XLA Modules:
  0.0 43.1 jit_solution(12370997657302783048)
XLA Ops:
  0.0 0.0 copy-start.1
  0.0 0.0 copy-start.2
  0.0 0.0 copy-start
  0.0 0.0 copy-start.3
  0.0 5.1 %shard_map.82 = (bf16[144,256]{1,0:T(8,128)(2,1)S(1)}, bf16[512,256]{1,0:T(8,128)(2,1)S(1)}) custom-call(s32[1,128]{1,0:T(1,128)} %bitcast.9, s32[1,128]{1,0:T(1,128)} %row_ref.1, bf16[128,1024]{1,0:T(8,128)(2,1)} %table_ref.1, bf16[1024,4,256]{2,1,0:T(4,128)(2,1)} %weight_hbm.1), custom_call_target="tpu_custom_call" | custom-call | tf_op jit(solution)/shard_map/pallas_call | solution.py:41
  5.1 3.0 %collective-permute-start.3 = (bf16[512,256]{1,0:T(8,128)(2,1)S(1)}, bf16[512,256]{1,0:T(8,128)(2,1)S(1)}, u32[]{:S(2)}, u32[]{:S(2)}) collective-permute-start(bf16[512,256]{1,0:T(8,128)(2,1)S(1)} %get-tuple-element.24.refs_4_), channel_id=1, source_target_pairs={{0,16},{16,0},{1,17},{17,1},{2,18},{18,2},{3,19},{19,3},{4,20},{20... | collective-permute-start | bytes 786440 | tf_op jit(solution)/shard_map/ppermute | solution.py:271
  8.2 1.6 %collective-permute-start = (bf16[144,256]{1,0:T(8,128)(2,1)S(1)}, bf16[144,256]{1,0:T(8,128)(2,1)S(1)}, u32[]{:S(2)}, u32[]{:S(2)}) collective-permute-start(bf16[144,256]{1,0:T(8,128)(2,1)S(1)} %get-tuple-element.23.refs_0_), channel_id=1, source_target_pairs={{0,4},{4,0},{8,12},{12,8},{1,5},{5,1},{9,13},{13,9},{2,6},{6,2},{1... | collective-permute-start | bytes 221192 | tf_op jit(solution)/shard_map/ppermute | solution.py:271
  9.7 2.6 %collective-permute-start.1 = (bf16[144,256]{1,0:T(8,128)(2,1)S(1)}, bf16[144,256]{1,0:T(8,128)(2,1)S(1)}, u32[]{:S(2)}, u32[]{:S(2)}) collective-permute-start(bf16[144,256]{1,0:T(8,128)(2,1)S(1)} %get-tuple-element.23.refs_0_), channel_id=1, source_target_pairs={{0,8},{4,12},{8,0},{12,4},{1,9},{5,13},{9,1},{13,5},{2,10},{6,14},... | collective-permute-start | bytes 221192 | tf_op jit(solution)/shard_map/ppermute | solution.py:271
  12.3 0.2 collective-permute-start.2
  12.5 0.0 collective-permute-done.refs_1_
  12.5 0.3 collective-permute-start.4
  12.9 4.4 %collective-permute-done.1.refs_2_ = bf16[144,256]{1,0:T(8,128)(2,1)S(1)} collective-permute-done((bf16[144,256]{1,0:T(8,128)(2,1)S(1)}, bf16[144,256]{1,0:T(8,128)(2,1)S(1)}, u32[]{:S(2)}, u32[]{:S(2)}) %collective-permute-start.1) | collective-permute-done | bytes 73760 | tf_op jit(solution)/shard_map/ppermute | solution.py:271
  17.2 0.5 %collective-permute-start.5 = (bf16[144,256]{1,0:T(8,128)(2,1)S(1)}, bf16[144,256]{1,0:T(8,128)(2,1)S(1)}, u32[]{:S(2)}, u32[]{:S(2)}) collective-permute-start(bf16[144,256]{1,0:T(8,128)(2,1)S(1)} %collective-permute-done.1.refs_2_), channel_id=1, source_target_pairs={{0,16},{16,0},{1,17},{17,1},{2,18},{18,2},{3,19},{19,3},{4,20},{20... | collective-permute-start | bytes 221192 | tf_op jit(solution)/shard_map/ppermute | solution.py:271
  17.8 0.8 %collective-permute-done.2.refs_3_ = bf16[144,256]{1,0:T(8,128)(2,1)S(1)} collective-permute-done((bf16[144,256]{1,0:T(8,128)(2,1)S(1)}, bf16[144,256]{1,0:T(8,128)(2,1)S(1)}, u32[]{:S(2)}, u32[]{:S(2)}) %collective-permute-start.2) | collective-permute-done | bytes 73760 | tf_op jit(solution)/shard_map/ppermute | solution.py:271
  18.6 0.7 %collective-permute-start.6 = (bf16[144,256]{1,0:T(8,128)(2,1)S(1)}, bf16[144,256]{1,0:T(8,128)(2,1)S(1)}, u32[]{:S(2)}, u32[]{:S(2)}) collective-permute-start(bf16[144,256]{1,0:T(8,128)(2,1)S(1)} %collective-permute-done.2.refs_3_), channel_id=1, source_target_pairs={{0,16},{16,0},{1,17},{17,1},{2,18},{18,2},{3,19},{19,3},{4,20},{20... | collective-permute-start | bytes 221192 | tf_op jit(solution)/shard_map/ppermute | solution.py:271
  19.3 0.0 collective-permute-done.3.refs_5_.refs_8_
  19.3 1.9 %shard_map.83 = (bf16[128,256]{1,0:T(8,128)(2,1)S(1)}, bf16[128,256]{1,0:T(8,128)(2,1)S(1)}, bf16[128,256]{1,0:T(8,128)(2,1)S(1)}, bf16[128,512]{1,0:T(8,128)(2,...) custom-call(bf16[144,256]{1,0:T(8,128)(2,1)S(1)} %get-tuple-element.23.refs_0_, ...), custom_call_target="tpu_custom_call" | custom-call | tf_op jit(solution)/shard_map/pallas_call | solution.py:41
  21.1 0.0 collective-permute-done.4.refs_9_
  21.2 0.4 %collective-permute-done.5.refs_10_ = bf16[144,256]{1,0:T(8,128)(2,1)S(1)} collective-permute-done((bf16[144,256]{1,0:T(8,128)(2,1)S(1)}, bf16[144,256]{1,0:T(8,128)(2,1)S(1)}, u32[]{:S(2)}, u32[]{:S(2)}) %collective-permute-start.5) | collective-permute-done | bytes 73760 | tf_op jit(solution)/shard_map/ppermute | solution.py:271
  21.6 1.3 %collective-permute-done.6.refs_11_ = bf16[144,256]{1,0:T(8,128)(2,1)S(1)} collective-permute-done((bf16[144,256]{1,0:T(8,128)(2,1)S(1)}, bf16[144,256]{1,0:T(8,128)(2,1)S(1)}, u32[]{:S(2)}, u32[]{:S(2)}) %collective-permute-start.6) | collective-permute-done | bytes 73760 | tf_op jit(solution)/shard_map/ppermute | solution.py:271
  22.9 0.0 copy-done.1
  22.9 0.0 copy-done.2
  22.9 1.2 %shard_map.84 = (bf16[128,256]{1,0:T(8,128)(2,1)S(1)}, bf16[256,256]{1,0:T(8,128)(2,1)S(1)}, bf16[256,256]{1,0:T(8,128)(2,1)S(1)}, bf16[256,256]{1,0:T(8,128)(2,1)S(1)}) custom-call(f32[512,128]{1,0:T(8,128)S(1)} %get-tuple-element.26.refs_0_, bf16[512,256]{1,0:T(8,128)(2,1)S(1)} %get-tuple-element.27.refs_1_, ...), custom_call_target="tpu_custom_call" | custom-call | tf_op jit(solution)/shard_map/pallas_call | solution.py:41
  24.1 0.9 %collective-permute-start.7 = (bf16[256,256]{1,0:T(8,128)(2,1)S(1)}, bf16[256,256]{1,0:T(8,128)(2,1)S(1)}, u32[]{:S(2)}, u32[]{:S(2)}) collective-permute-start(bf16[256,256]{1,0:T(8,128)(2,1)S(1)} %get-tuple-element.33), channel_id=1, source_target_pairs={{0,4},{4,0},{8,12},{12,8},{1,5},{5,1},{9,13},{13,9},{2,6},{6,2},{1... | collective-permute-start | bytes 393224 | tf_op jit(solution)/shard_map/ppermute | solution.py:271
  25.0 2.5 %collective-permute-start.8 = (bf16[256,256]{1,0:T(8,128)(2,1)S(1)}, bf16[256,256]{1,0:T(8,128)(2,1)S(1)}, u32[]{:S(2)}, u32[]{:S(2)}) collective-permute-start(bf16[256,256]{1,0:T(8,128)(2,1)S(1)} %get-tuple-element.34), channel_id=1, source_target_pairs={{0,8},{4,12},{8,0},{12,4},{1,9},{5,13},{9,1},{13,5},{2,10},{6,14},... | collective-permute-start | bytes 393224 | tf_op jit(solution)/shard_map/ppermute | solution.py:271
  27.5 1.1 %collective-permute-start.9 = (bf16[256,256]{1,0:T(8,128)(2,1)S(1)}, bf16[256,256]{1,0:T(8,128)(2,1)S(1)}, u32[]{:S(2)}, u32[]{:S(2)}) collective-permute-start(bf16[256,256]{1,0:T(8,128)(2,1)S(1)} %get-tuple-element.35), channel_id=1, source_target_pairs={{0,12},{4,8},{8,4},{12,0},{1,13},{5,9},{9,5},{13,1},{2,14},{6,10},... | collective-permute-start | bytes 393224 | tf_op jit(solution)/shard_map/ppermute | solution.py:271
  29.3 1.1 %collective-permute-done.7.refs_4_ = bf16[256,256]{1,0:T(8,128)(2,1)S(1)} collective-permute-done((bf16[256,256]{1,0:T(8,128)(2,1)S(1)}, bf16[256,256]{1,0:T(8,128)(2,1)S(1)}, u32[]{:S(2)}, u32[]{:S(2)}) %collective-permute-start.7) | collective-permute-done | bytes 131104 | tf_op jit(solution)/shard_map/ppermute | solution.py:271
  30.4 5.4 %collective-permute-done.8.refs_5_ = bf16[256,256]{1,0:T(8,128)(2,1)S(1)} collective-permute-done((bf16[256,256]{1,0:T(8,128)(2,1)S(1)}, bf16[256,256]{1,0:T(8,128)(2,1)S(1)}, u32[]{:S(2)}, u32[]{:S(2)}) %collective-permute-start.8) | collective-permute-done | bytes 131104 | tf_op jit(solution)/shard_map/ppermute | solution.py:271
  35.7 0.0 collective-permute-done.9.refs_6_
  35.7 0.0 copy-done
  35.7 0.0 copy-done.3
  35.7 0.8 %shard_map.85 = (f32[128,256]{1,0:T(8,128)S(1)}, bf16[128,256]{1,0:T(8,128)(2,1)S(1)}, bf16[128,256]{1,0:T(8,128)(2,1)S(1)}, bf16[128,256]{1,0:T(8,128)(2,1)S(1)}, bf16[128,256]{1,0:T(8,128)(2,1)S(1)}) custom-call(s32[1,128]{1,0:T(1,128)S(1)} %bitcast.10, bf16[128,512]{1,0:T(8,128)(2,1)S(1)} %get-tuple-element.25.refs_1_, bf16[256,1024]{1,0:T(8,128)(2,1)S(1)} %copy-done, ...), custom_call_target="tpu_custom_call" | custom-call | tf_op jit(solution)/shard_map/pallas_call | solution.py:41
  36.6 0.1 collective-permute-start.12
  36.6 1.6 %collective-permute-start.11 = (bf16[128,256]{1,0:T(8,128)(2,1)S(1)}, bf16[128,256]{1,0:T(8,128)(2,1)S(1)}, u32[]{:S(2)}, u32[]{:S(2)}) collective-permute-start(bf16[128,256]{1,0:T(8,128)(2,1)S(1)} %get-tuple-element.39), channel_id=1, source_target_pairs={{0,2},{1,3},{2,0},{3,1},{4,6},{5,7},{6,4},{7,5},{8,10},{9,11},{10,... | collective-permute-start | bytes 196616 | tf_op jit(solution)/shard_map/ppermute | solution.py:271
  38.2 0.3 collective-permute-start.10
  38.5 2.4 %collective-permute-done.12 = bf16[128,256]{1,0:T(8,128)(2,1)S(1)} collective-permute-done((bf16[128,256]{1,0:T(8,128)(2,1)S(1)}, bf16[128,256]{1,0:T(8,128)(2,1)S(1)}, u32[]{:S(2)}, u32[]{:S(2)}) %collective-permute-start.12) | collective-permute-done | bytes 65568 | tf_op jit(solution)/shard_map/ppermute | solution.py:271
  40.9 1.5 %collective-permute-done.11 = bf16[128,256]{1,0:T(8,128)(2,1)S(1)} collective-permute-done((bf16[128,256]{1,0:T(8,128)(2,1)S(1)}, bf16[128,256]{1,0:T(8,128)(2,1)S(1)}, u32[]{:S(2)}, u32[]{:S(2)}) %collective-permute-start.11) | collective-permute-done | bytes 65568 | tf_op jit(solution)/shard_map/ppermute | solution.py:271
  42.4 0.0 collective-permute-done.10
  42.4 0.7 %fusion = bf16[1,128,256]{2,1,0:T(8,128)(2,1)} fusion(bf16[128,256]{1,0:T(8,128)(2,1)S(1)} %collective-permute-done.12, bf16[128,256]{1,0:T(8,128)(2,1)S(1)} %collective-permute-done.11, bf16[128,256]{1,0:T(8,128)(2,1)S(1)} %collective-permute-done.10, f32[128,256]{1,0:T(8,128)S(1)} %get-tuple-element.37, bf16[128,256]{1,0:T(8,128)(2,1)S(1)} %get-tuple-element.36, ...), kind=kLoop, calls=%fused_computation.1 | loop fusion | flops 327680 | bytes 458880 | tf_op jit(solution)/shard_map/broadcast_in_dim | solution.py:337
  (1 shorter events, 0.0 us)
Async XLA Ops:
  0.0 22.9 %copy-start.1 = (bf16[1,512,256]{2,1,0:T(8,128)(2,1)S(1)}, bf16[1,512,256]{2,1,0:T(8,128)(2,1)}, u32[]{:S(2)}) copy-start(bf16[1,512,256]{2,1,0:T(8,128)(2,1)} %param.14) | copy-start | bytes 786436
  0.0 22.9 %copy-start.2 = (bf16[1,512,256]{2,1,0:T(8,128)(2,1)S(1)}, bf16[1,512,256]{2,1,0:T(8,128)(2,1)}, u32[]{:S(2)}) copy-start(bf16[1,512,256]{2,1,0:T(8,128)(2,1)} %param.15) | copy-start | bytes 786436
  0.0 35.7 %copy-start = (bf16[256,1024]{1,0:T(8,128)(2,1)S(1)}, bf16[256,1024]{1,0:T(8,128)(2,1)}, u32[]{:S(2)}) copy-start(bf16[256,1024]{1,0:T(8,128)(2,1)} %refs_2_.1) | copy-start | bytes 1572868
  0.0 35.7 %copy-start.3 = (s32[1,128,1]{1,2,0:T(1,128)S(1)}, s32[1,128,1]{1,2,0:T(1,128)}, u32[]{:S(2)}) copy-start(s32[1,128,1]{1,2,0:T(1,128)} %param.9) | copy-start | bytes 1540
  5.1 14.2 %collective-permute-start.3 = (bf16[512,256]{1,0:T(8,128)(2,1)S(1)}, bf16[512,256]{1,0:T(8,128)(2,1)S(1)}, u32[]{:S(2)}, u32[]{:S(2)}) collective-permute-start(bf16[512,256]{1,0:T(8,128)(2,1)S(1)} %get-tuple-element.24.refs_4_), channel_id=1, source_target_pairs={{0,16},{16,0},{1,17},{17,1},{2,18},{18,2},{3,19},{19,3},{4,20},{20... | collective-permute-start | bytes 786440 | tf_op jit(solution)/shard_map/ppermute | solution.py:271
  8.2 4.4 %collective-permute-start = (bf16[144,256]{1,0:T(8,128)(2,1)S(1)}, bf16[144,256]{1,0:T(8,128)(2,1)S(1)}, u32[]{:S(2)}, u32[]{:S(2)}) collective-permute-start(bf16[144,256]{1,0:T(8,128)(2,1)S(1)} %get-tuple-element.23.refs_0_), channel_id=1, source_target_pairs={{0,4},{4,0},{8,12},{12,8},{1,5},{5,1},{9,13},{13,9},{2,6},{6,2},{1... | collective-permute-start | bytes 221192 | tf_op jit(solution)/shard_map/ppermute | solution.py:271
  9.7 7.5 %collective-permute-start.1 = (bf16[144,256]{1,0:T(8,128)(2,1)S(1)}, bf16[144,256]{1,0:T(8,128)(2,1)S(1)}, u32[]{:S(2)}, u32[]{:S(2)}) collective-permute-start(bf16[144,256]{1,0:T(8,128)(2,1)S(1)} %get-tuple-element.23.refs_0_), channel_id=1, source_target_pairs={{0,8},{4,12},{8,0},{12,4},{1,9},{5,13},{9,1},{13,5},{2,10},{6,14},... | collective-permute-start | bytes 221192 | tf_op jit(solution)/shard_map/ppermute | solution.py:271
  12.3 6.3 %collective-permute-start.2 = (bf16[144,256]{1,0:T(8,128)(2,1)S(1)}, bf16[144,256]{1,0:T(8,128)(2,1)S(1)}, u32[]{:S(2)}, u32[]{:S(2)}) collective-permute-start(bf16[144,256]{1,0:T(8,128)(2,1)S(1)} %get-tuple-element.23.refs_0_), channel_id=1, source_target_pairs={{0,12},{4,8},{8,4},{12,0},{1,13},{5,9},{9,5},{13,1},{2,14},{6,10},... | collective-permute-start | bytes 221192 | tf_op jit(solution)/shard_map/ppermute | solution.py:271
  12.5 8.6 %collective-permute-start.4 = (bf16[144,256]{1,0:T(8,128)(2,1)S(1)}, bf16[144,256]{1,0:T(8,128)(2,1)S(1)}, u32[]{:S(2)}, u32[]{:S(2)}) collective-permute-start(bf16[144,256]{1,0:T(8,128)(2,1)S(1)} %collective-permute-done.refs_1_), channel_id=1, source_target_pairs={{0,16},{16,0},{1,17},{17,1},{2,18},{18,2},{3,19},{19,3},{4,20},{20... | collective-permute-start | bytes 221192 | tf_op jit(solution)/shard_map/ppermute | solution.py:271
  17.2 4.4 %collective-permute-start.5 = (bf16[144,256]{1,0:T(8,128)(2,1)S(1)}, bf16[144,256]{1,0:T(8,128)(2,1)S(1)}, u32[]{:S(2)}, u32[]{:S(2)}) collective-permute-start(bf16[144,256]{1,0:T(8,128)(2,1)S(1)} %collective-permute-done.1.refs_2_), channel_id=1, source_target_pairs={{0,16},{16,0},{1,17},{17,1},{2,18},{18,2},{3,19},{19,3},{4,20},{20... | collective-permute-start | bytes 221192 | tf_op jit(solution)/shard_map/ppermute | solution.py:271
  18.6 4.4 %collective-permute-start.6 = (bf16[144,256]{1,0:T(8,128)(2,1)S(1)}, bf16[144,256]{1,0:T(8,128)(2,1)S(1)}, u32[]{:S(2)}, u32[]{:S(2)}) collective-permute-start(bf16[144,256]{1,0:T(8,128)(2,1)S(1)} %collective-permute-done.2.refs_3_), channel_id=1, source_target_pairs={{0,16},{16,0},{1,17},{17,1},{2,18},{18,2},{3,19},{19,3},{4,20},{20... | collective-permute-start | bytes 221192 | tf_op jit(solution)/shard_map/ppermute | solution.py:271
  24.1 6.2 %collective-permute-start.7 = (bf16[256,256]{1,0:T(8,128)(2,1)S(1)}, bf16[256,256]{1,0:T(8,128)(2,1)S(1)}, u32[]{:S(2)}, u32[]{:S(2)}) collective-permute-start(bf16[256,256]{1,0:T(8,128)(2,1)S(1)} %get-tuple-element.33), channel_id=1, source_target_pairs={{0,4},{4,0},{8,12},{12,8},{1,5},{5,1},{9,13},{13,9},{2,6},{6,2},{1... | collective-permute-start | bytes 393224 | tf_op jit(solution)/shard_map/ppermute | solution.py:271
  25.0 10.7 %collective-permute-start.8 = (bf16[256,256]{1,0:T(8,128)(2,1)S(1)}, bf16[256,256]{1,0:T(8,128)(2,1)S(1)}, u32[]{:S(2)}, u32[]{:S(2)}) collective-permute-start(bf16[256,256]{1,0:T(8,128)(2,1)S(1)} %get-tuple-element.34), channel_id=1, source_target_pairs={{0,8},{4,12},{8,0},{12,4},{1,9},{5,13},{9,1},{13,5},{2,10},{6,14},... | collective-permute-start | bytes 393224 | tf_op jit(solution)/shard_map/ppermute | solution.py:271
  27.5 8.3 %collective-permute-start.9 = (bf16[256,256]{1,0:T(8,128)(2,1)S(1)}, bf16[256,256]{1,0:T(8,128)(2,1)S(1)}, u32[]{:S(2)}, u32[]{:S(2)}) collective-permute-start(bf16[256,256]{1,0:T(8,128)(2,1)S(1)} %get-tuple-element.35), channel_id=1, source_target_pairs={{0,12},{4,8},{8,4},{12,0},{1,13},{5,9},{9,5},{13,1},{2,14},{6,10},... | collective-permute-start | bytes 393224 | tf_op jit(solution)/shard_map/ppermute | solution.py:271
  36.6 4.4 %collective-permute-start.12 = (bf16[128,256]{1,0:T(8,128)(2,1)S(1)}, bf16[128,256]{1,0:T(8,128)(2,1)S(1)}, u32[]{:S(2)}, u32[]{:S(2)}) collective-permute-start(bf16[128,256]{1,0:T(8,128)(2,1)S(1)} %get-tuple-element.40), channel_id=1, source_target_pairs={{0,3},{1,2},{2,1},{3,0},{4,7},{5,6},{6,5},{7,4},{8,11},{9,10},{10,... | collective-permute-start | bytes 196616 | tf_op jit(solution)/shard_map/ppermute | solution.py:271
  36.6 5.8 %collective-permute-start.11 = (bf16[128,256]{1,0:T(8,128)(2,1)S(1)}, bf16[128,256]{1,0:T(8,128)(2,1)S(1)}, u32[]{:S(2)}, u32[]{:S(2)}) collective-permute-start(bf16[128,256]{1,0:T(8,128)(2,1)S(1)} %get-tuple-element.39), channel_id=1, source_target_pairs={{0,2},{1,3},{2,0},{3,1},{4,6},{5,7},{6,4},{7,5},{8,10},{9,11},{10,... | collective-permute-start | bytes 196616 | tf_op jit(solution)/shard_map/ppermute | solution.py:271
  38.2 4.2 %collective-permute-start.10 = (bf16[128,256]{1,0:T(8,128)(2,1)S(1)}, bf16[128,256]{1,0:T(8,128)(2,1)S(1)}, u32[]{:S(2)}, u32[]{:S(2)}) collective-permute-start(bf16[128,256]{1,0:T(8,128)(2,1)S(1)} %get-tuple-element.38), channel_id=1, source_target_pairs={{0,1},{1,0},{2,3},{3,2},{4,5},{5,4},{6,7},{7,6},{8,9},{9,8},{10,11... | collective-permute-start | bytes 196616 | tf_op jit(solution)/shard_map/ppermute | solution.py:271

commit v2 on v1

--- a/solution.py
+++ b/solution.py
@@ -182,9 +182,8 @@
 
 def attend_kernel(users, ctx_size, rows, history, places, *refs):
     spot_ref, part_ref, own_ref, key_ref, value_ref = refs[:5]
-    packs = refs[5 : 4 + ctx_size]
     outs = refs[-ctx_size - 2 : -2]
-    others = refs[4 + ctx_size : -ctx_size - 2]
+    others = refs[5 : -ctx_size - 2]
     query_ref, sum_ref = refs[-2:]
     width = key_ref.shape[1]
     slots = outs[0].shape[0]
@@ -217,16 +216,15 @@
     loop(count // block, attend)
     for j in range(ctx_size):
         span = slice(j * slots, (j + 1) * slots)
-        outs[j][0:slots, :] = (sum_ref[span, :] * history ** (-0.5) + own_ref[span, :].astype(F32)).astype(BF16)
-        if j > 0:
-            outs[j][slots:, :] = packs[j - 1][...]
+        outs[j][...] = (sum_ref[span, :] * history ** (-0.5) + own_ref[span, :].astype(F32)).astype(BF16)
 
 
 def mix_kernel(users, ctx_size, head_size, held, *refs):
     owner_ref, mine_ref, weight_ref = refs[:3]
     sums = refs[3 : 3 + ctx_size]
-    outs = refs[3 + ctx_size : 3 + ctx_size + head_size]
-    residual_ref = refs[3 + ctx_size + head_size]
+    packs = refs[3 + ctx_size : 2 + 2 * ctx_size]
+    outs = refs[2 + 2 * ctx_size : 2 + 2 * ctx_size + head_size]
+    residual_ref = refs[2 + 2 * ctx_size + head_size]
     me_user = lax.axis_index("users")
     me_ctx = lax.axis_index("ctx")
     me_head = lax.axis_index("head")
@@ -247,10 +245,10 @@
     residual = mine_ref[:, width:].astype(F32)
     spots = lax.broadcasted_iota(jnp.int32, (slots, held), 1).astype(F32)
     for m in range(1, ctx_size):
-        attended = attended + sums[m][0:slots, :].astype(F32)
+        attended = attended + sums[m][...].astype(F32)
         pick = (spots == rank[:, m : m + 1]).astype(F32).astype(BF16)
-        gates = gates + dot(pick, sums[m][slots : slots + held, :])
-        residual = residual + dot(pick, sums[m][slots + held :, :])
+        gates = gates + dot(pick, packs[m - 1][0:held, :])
+        residual = residual + dot(pick, packs[m - 1][held:, :])
     residual_ref[...] = residual.astype(BF16)
     parts = []
     for at in range(0, width, HEAD_DIM):
@@ -301,16 +299,11 @@
     for k in range(1, users):
         places[k, 0] = (len(relays), 3 * rows)
         relays.append(bulks[k])
-    if users * ctx_size <= 8:
-        for m in range(1, ctx_size):
-            for k in range(1, users):
-                places[k, m] = (len(relays), 0)
-                relays.append(swap(packets[m], "users", k))
-    elif ctx_size > 1:
-        joined = jnp.concatenate(packets[1:], axis=0)
+    if ctx_size > 1:
+        joined = jnp.concatenate([one[0:rows] for one in packets[1:]], axis=0)
         for k in range(1, users):
             for m in range(1, ctx_size):
-                places[k, m] = (len(relays), (m - 1) * span)
+                places[k, m] = (len(relays), (m - 1) * rows)
             relays.append(swap(joined, "users", k))
     count = ctx_size * slots
     *packs, mine, own, part, spots = call(
@@ -319,16 +312,17 @@
         + (shape((slots, 2 * width)), shape((count, width)), shape((count, width)), shape((count, 128), F32)),
         (pltpu.VMEM((ctx_size, width, PAD), F32),),
     )(*packets, *bulks)
+    packs = [swap(packs[m - 1], "ctx", m) for m in range(1, ctx_size)]
     sums = call(
         lambda *refs: attend_kernel(users, ctx_size, rows, history, places, *refs),
-        (shape((slots, width)),) + (shape((slots + 2 * held, width)),) * (ctx_size - 1),
+        (shape((slots, width)),) * ctx_size,
         (pltpu.VMEM((count, width), BF16), pltpu.VMEM((count, width), F32)),
-    )(spots, part, own, key_cache[0], value_cache[0], *packs, *relays)
+    )(spots, part, own, key_cache[0], value_cache[0], *relays)
     sums = [sums[0]] + [swap(sums[m], "ctx", m) for m in range(1, ctx_size)]
     *parts, residual = call(
         lambda *refs: mix_kernel(users, ctx_size, head_size, held, *refs),
         (shape((slots, width), F32),) + (shape((slots, width)),) * (head_size - 1) + (shape((slots, width)),),
-    )(owner, mine, out_weight, *sums)
+    )(owner, mine, out_weight, *sums, *packs)
     got = [parts[0]] + [swap(parts[t], "head", t) for t in range(1, head_size)]
     total = residual.astype(F32)
     for one in got:

time: 43.3 us -> 45.5 us (1.051)
  starting transfers between devices: 15.3 us -> 21.3 us
  waiting for transfers between devices: 17.4 us -> 13.6 us
    ppermute x13 -> x14, starting transfers between devices: 15.3 us -> 21.3 us  [swap(): lax.ppermute(x, axis, [(i, i ^ k) for i in range(lax.axis_size(axis))])]
    ppermute x13 -> x14, waiting for transfers between devices: 17.4 us -> 13.6 us  [swap(): lax.ppermute(x, axis, [(i, i ^ k) for i in range(lax.axis_size(axis))])]
  transfers between devices with their start and end apart: 13 -> 14, of which waited for: 8 -> 7; matrix products, arithmetic and copies ran while one was open for 0% -> 0% of each run, Pallas kernels for 4% -> 7%
where the time goes in v2:
time: 45.5 us; the launch traced here: 45.3 us
  starting transfers between devices  21.3 us (47%)
  waiting for transfers between devices  13.6 us (30%)
  Pallas kernels  8.93 us (20%)
  between operations  0.76 us (2%)
  other arithmetic  0.73 us (2%)
    ppermute x14, starting transfers between devices, swap(): lax.ppermute(x, axis, [(i, i ^ k) for i in range(lax.axis_size(axis))])  21.3 us
    ppermute x14, waiting for transfers between devices, swap(): lax.ppermute(x, axis, [(i, i ^ k) for i in range(lax.axis_size(axis))])  13.6 us
    pallas_call x4, Pallas kernels, run(): return made(*args)  8.93 us
  transfers between devices with their start and end apart: 14, of which 7 were waited for; matrix products, arithmetic and copies ran while one was open for 0% of the time, Pallas kernels for 7%

profile of v2, /device:TPU:0, one launch (start us, length us, event | category | flops | bytes accessed | tf_op | source)
XLA Modules:
  0.0 45.3 jit_solution(13461416644296157428)
XLA Ops:
  0.0 0.0 copy-start.1
  0.0 0.0 copy-start.2
  0.0 5.1 %shard_map.82 = (bf16[144,256]{1,0:T(8,128)(2,1)S(1)}, bf16[512,256]{1,0:T(8,128)(2,1)S(1)}) custom-call(s32[1,128]{1,0:T(1,128)} %bitcast.9, s32[1,128]{1,0:T(1,128)} %row_ref.1, bf16[128,1024]{1,0:T(8,128)(2,1)} %table_ref.1, bf16[1024,4,256]{2,1,0:T(4,128)(2,1)} %weight_hbm.1), custom_call_target="tpu_custom_call" | custom-call | tf_op jit(solution)/shard_map/pallas_call | solution.py:41
  5.1 0.0 copy-start
  5.1 0.0 copy-start.3
  5.1 3.1 %collective-permute-start = (bf16[144,256]{1,0:T(8,128)(2,1)S(1)}, bf16[144,256]{1,0:T(8,128)(2,1)S(1)}, u32[]{:S(2)}, u32[]{:S(2)}) collective-permute-start(bf16[144,256]{1,0:T(8,128)(2,1)S(1)} %get-tuple-element.23.refs_0_), channel_id=1, source_target_pairs={{0,4},{4,0},{8,12},{12,8},{1,5},{5,1},{9,13},{13,9},{2,6},{6,2},{1... | collective-permute-start | bytes 221192 | tf_op jit(solution)/shard_map/ppermute | solution.py:269
  8.2 2.6 %collective-permute-start.1 = (bf16[144,256]{1,0:T(8,128)(2,1)S(1)}, bf16[144,256]{1,0:T(8,128)(2,1)S(1)}, u32[]{:S(2)}, u32[]{:S(2)}) collective-permute-start(bf16[144,256]{1,0:T(8,128)(2,1)S(1)} %get-tuple-element.23.refs_0_), channel_id=1, source_target_pairs={{0,8},{4,12},{8,0},{12,4},{1,9},{5,13},{9,1},{13,5},{2,10},{6,14},... | collective-permute-start | bytes 221192 | tf_op jit(solution)/shard_map/ppermute | solution.py:269
  10.8 0.0 collective-permute-start.2
  10.8 1.7 %collective-permute-start.3 = (bf16[512,256]{1,0:T(8,128)(2,1)S(1)}, bf16[512,256]{1,0:T(8,128)(2,1)S(1)}, u32[]{:S(2)}, u32[]{:S(2)}) collective-permute-start(bf16[512,256]{1,0:T(8,128)(2,1)S(1)} %get-tuple-element.24.refs_4_), channel_id=1, source_target_pairs={{0,16},{16,0},{1,17},{17,1},{2,18},{18,2},{3,19},{19,3},{4,20},{20... | collective-permute-start | bytes 786440 | tf_op jit(solution)/shard_map/ppermute | solution.py:269
  12.5 0.0 collective-permute-done.refs_1_
  12.5 3.5 %collective-permute-done.1.refs_2_ = bf16[144,256]{1,0:T(8,128)(2,1)S(1)} collective-permute-done((bf16[144,256]{1,0:T(8,128)(2,1)S(1)}, bf16[144,256]{1,0:T(8,128)(2,1)S(1)}, u32[]{:S(2)}, u32[]{:S(2)}) %collective-permute-start.1) | collective-permute-done | bytes 73760 | tf_op jit(solution)/shard_map/ppermute | solution.py:269
  16.0 1.0 %collective-permute-done.2.refs_3_ = bf16[144,256]{1,0:T(8,128)(2,1)S(1)} collective-permute-done((bf16[144,256]{1,0:T(8,128)(2,1)S(1)}, bf16[144,256]{1,0:T(8,128)(2,1)S(1)}, u32[]{:S(2)}, u32[]{:S(2)}) %collective-permute-start.2) | collective-permute-done | bytes 73760 | tf_op jit(solution)/shard_map/ppermute | solution.py:269
  17.1 1.6 %collective-permute-start.4 = (bf16[384,256]{1,0:T(8,128)(2,1)S(1)}, bf16[384,256]{1,0:T(8,128)(2,1)S(1)}, u32[]{:S(2)}, u32[]{:S(2)}) collective-permute-start(bf16[384,256]{1,0:T(8,128)(2,1)S(1)} %pad_maximum_fusion), channel_id=1, source_target_pairs={{0,16},{16,0},{1,17},{17,1},{2,18},{18,2},{3,19},{19,3},{4,20},{20... | collective-permute-start | bytes 589832 | tf_op jit(solution)/shard_map/ppermute | solution.py:269
  18.6 0.2 collective-permute-done.3.refs_5_
  18.8 1.9 %shard_map.83 = (bf16[128,256]{1,0:T(8,128)(2,1)S(1)}, bf16[128,256]{1,0:T(8,128)(2,1)S(1)}, bf16[128,256]{1,0:T(8,128)(2,1)S(1)}, bf16[128,512]{1,0:T(8,128)(2,...) custom-call(bf16[144,256]{1,0:T(8,128)(2,1)S(1)} %get-tuple-element.23.refs_0_, ...), custom_call_target="tpu_custom_call" | custom-call | tf_op jit(solution)/shard_map/pallas_call | solution.py:41
  20.7 5.1 %collective-permute-start.10 = (bf16[128,256]{1,0:T(8,128)(2,1)S(1)}, bf16[128,256]{1,0:T(8,128)(2,1)S(1)}, u32[]{:S(2)}, u32[]{:S(2)}) collective-permute-start(bf16[128,256]{1,0:T(8,128)(2,1)S(1)} %get-tuple-element.35), channel_id=1, source_target_pairs={{0,12},{4,8},{8,4},{12,0},{1,13},{5,9},{9,5},{13,1},{2,14},{6,10},... | collective-permute-start | bytes 196616 | tf_op jit(solution)/shard_map/ppermute | solution.py:269
  25.8 0.0 collective-permute-start.8
  25.8 0.6 %collective-permute-start.9 = (bf16[128,256]{1,0:T(8,128)(2,1)S(1)}, bf16[128,256]{1,0:T(8,128)(2,1)S(1)}, u32[]{:S(2)}, u32[]{:S(2)}) collective-permute-start(bf16[128,256]{1,0:T(8,128)(2,1)S(1)} %get-tuple-element.34), channel_id=1, source_target_pairs={{0,8},{4,12},{8,0},{12,4},{1,9},{5,13},{9,1},{13,5},{2,10},{6,14},... | collective-permute-start | bytes 196616 | tf_op jit(solution)/shard_map/ppermute | solution.py:269
  26.4 0.0 collective-permute-done.4.refs_6_
  26.4 0.0 copy-done.1
  26.4 0.0 copy-done.2
  26.4 1.2 %shard_map.84 = (bf16[128,256]{1,0:T(8,128)(2,1)S(1)}, bf16[128,256]{1,0:T(8,128)(2,1)S(1)}, bf16[128,256]{1,0:T(8,128)(2,1)S(1)}, bf16[128,256]{1,0:T(8,128)(2,1)S(1)}) custom-call(f32[512,128]{1,0:T(8,128)S(1)} %get-tuple-element.26.refs_0_, bf16[512,256]{1,0:T(8,128)(2,1)S(1)} %get-tuple-element.27.refs_1_, ...), custom_call_target="tpu_custom_call" | custom-call | tf_op jit(solution)/shard_map/pallas_call | solution.py:41
  27.6 1.5 %collective-permute-start.5 = (bf16[128,256]{1,0:T(8,128)(2,1)S(1)}, bf16[128,256]{1,0:T(8,128)(2,1)S(1)}, u32[]{:S(2)}, u32[]{:S(2)}) collective-permute-start(bf16[128,256]{1,0:T(8,128)(2,1)S(1)} %get-tuple-element.30), channel_id=1, source_target_pairs={{0,4},{4,0},{8,12},{12,8},{1,5},{5,1},{9,13},{13,9},{2,6},{6,2},{1... | collective-permute-start | bytes 196616 | tf_op jit(solution)/shard_map/ppermute | solution.py:269
  29.1 2.9 %collective-permute-start.6 = (bf16[128,256]{1,0:T(8,128)(2,1)S(1)}, bf16[128,256]{1,0:T(8,128)(2,1)S(1)}, u32[]{:S(2)}, u32[]{:S(2)}) collective-permute-start(bf16[128,256]{1,0:T(8,128)(2,1)S(1)} %get-tuple-element.31), channel_id=1, source_target_pairs={{0,8},{4,12},{8,0},{12,4},{1,9},{5,13},{9,1},{13,5},{2,10},{6,14},... | collective-permute-start | bytes 196616 | tf_op jit(solution)/shard_map/ppermute | solution.py:269
  32.0 0.0 collective-permute-done.10.refs_9_
  32.0 0.3 collective-permute-start.7
  33.0 0.0 collective-permute-done.8.refs_7_
  33.0 0.0 collective-permute-done.9.refs_8_
  33.0 0.0 collective-permute-done.5.refs_4_
  33.0 2.0 %collective-permute-done.6.refs_5_ = bf16[128,256]{1,0:T(8,128)(2,1)S(1)} collective-permute-done((bf16[128,256]{1,0:T(8,128)(2,1)S(1)}, bf16[128,256]{1,0:T(8,128)(2,1)S(1)}, u32[]{:S(2)}, u32[]{:S(2)}) %collective-permute-start.6) | collective-permute-done | bytes 65568 | tf_op jit(solution)/shard_map/ppermute | solution.py:269
  34.9 3.1 %collective-permute-done.7.refs_6_ = bf16[128,256]{1,0:T(8,128)(2,1)S(1)} collective-permute-done((bf16[128,256]{1,0:T(8,128)(2,1)S(1)}, bf16[128,256]{1,0:T(8,128)(2,1)S(1)}, u32[]{:S(2)}, u32[]{:S(2)}) %collective-permute-start.7) | collective-permute-done | bytes 65568 | tf_op jit(solution)/shard_map/ppermute | solution.py:269
  38.1 0.0 copy-done
  38.1 0.0 copy-done.3
  38.1 0.8 %shard_map.85 = (f32[128,256]{1,0:T(8,128)S(1)}, bf16[128,256]{1,0:T(8,128)(2,1)S(1)}, bf16[128,256]{1,0:T(8,128)(2,1)S(1)}, bf16[128,256]{1,0:T(8,128)(2,1)S(1)}, bf16[128,256]{1,0:T(8,128)(2,1)S(1)}) custom-call(s32[1,128]{1,0:T(1,128)S(1)} %bitcast.10, bf16[128,512]{1,0:T(8,128)(2,1)S(1)} %get-tuple-element.25.refs_1_, bf16[256,1024]{1,0:T(8,128)(2,1)S(1)} %copy-done, ...), custom_call_target="tpu_custom_call" | custom-call | tf_op jit(solution)/shard_map/pallas_call | solution.py:41
  38.9 0.1 collective-permute-start.11
  38.9 1.6 %collective-permute-start.12 = (bf16[128,256]{1,0:T(8,128)(2,1)S(1)}, bf16[128,256]{1,0:T(8,128)(2,1)S(1)}, u32[]{:S(2)}, u32[]{:S(2)}) collective-permute-start(bf16[128,256]{1,0:T(8,128)(2,1)S(1)} %get-tuple-element.39), channel_id=1, source_target_pairs={{0,2},{1,3},{2,0},{3,1},{4,6},{5,7},{6,4},{7,5},{8,10},{9,11},{10,... | collective-permute-start | bytes 196616 | tf_op jit(solution)/shard_map/ppermute | solution.py:269
  40.5 0.3 collective-permute-start.13
  40.8 0.0 collective-permute-done.11
  40.8 2.6 %collective-permute-done.12 = bf16[128,256]{1,0:T(8,128)(2,1)S(1)} collective-permute-done((bf16[128,256]{1,0:T(8,128)(2,1)S(1)}, bf16[128,256]{1,0:T(8,128)(2,1)S(1)}, u32[]{:S(2)}, u32[]{:S(2)}) %collective-permute-start.12) | collective-permute-done | bytes 65568 | tf_op jit(solution)/shard_map/ppermute | solution.py:269
  43.4 1.1 %collective-permute-done.13 = bf16[128,256]{1,0:T(8,128)(2,1)S(1)} collective-permute-done((bf16[128,256]{1,0:T(8,128)(2,1)S(1)}, bf16[128,256]{1,0:T(8,128)(2,1)S(1)}, u32[]{:S(2)}, u32[]{:S(2)}) %collective-permute-start.13) | collective-permute-done | bytes 65568 | tf_op jit(solution)/shard_map/ppermute | solution.py:269
  44.6 0.7 %fusion = bf16[1,128,256]{2,1,0:T(8,128)(2,1)} fusion(bf16[128,256]{1,0:T(8,128)(2,1)S(1)} %collective-permute-done.13, bf16[128,256]{1,0:T(8,128)(2,1)S(1)} %collective-permute-done.12, bf16[128,256]{1,0:T(8,128)(2,1)S(1)} %collective-permute-done.11, f32[128,256]{1,0:T(8,128)S(1)} %get-tuple-element.37, bf16[128,256]{1,0:T(8,128)(2,1)S(1)} %get-tuple-element.36, ...), kind=kLoop, calls=%fused_computation.2 | loop fusion | flops 327680 | bytes 458880 | tf_op jit(solution)/shard_map/broadcast_in_dim | solution.py:331
  (5 shorter events, 0.0 us)
Async XLA Ops:
  0.0 26.4 %copy-start.1 = (bf16[1,512,256]{2,1,0:T(8,128)(2,1)S(1)}, bf16[1,512,256]{2,1,0:T(8,128)(2,1)}, u32[]{:S(2)}) copy-start(bf16[1,512,256]{2,1,0:T(8,128)(2,1)} %param.14) | copy-start | bytes 786436
  0.0 26.4 %copy-start.2 = (bf16[1,512,256]{2,1,0:T(8,128)(2,1)S(1)}, bf16[1,512,256]{2,1,0:T(8,128)(2,1)}, u32[]{:S(2)}) copy-start(bf16[1,512,256]{2,1,0:T(8,128)(2,1)} %param.15) | copy-start | bytes 786436
  5.1 33.0 %copy-start = (bf16[256,1024]{1,0:T(8,128)(2,1)S(1)}, bf16[256,1024]{1,0:T(8,128)(2,1)}, u32[]{:S(2)}) copy-start(bf16[256,1024]{1,0:T(8,128)(2,1)} %refs_2_.1) | copy-start | bytes 1572868
  5.1 33.0 %copy-start.3 = (s32[1,128,1]{1,2,0:T(1,128)S(1)}, s32[1,128,1]{1,2,0:T(1,128)}, u32[]{:S(2)}) copy-start(s32[1,128,1]{1,2,0:T(1,128)} %param.9) | copy-start | bytes 1540
  5.1 7.4 %collective-permute-start = (bf16[144,256]{1,0:T(8,128)(2,1)S(1)}, bf16[144,256]{1,0:T(8,128)(2,1)S(1)}, u32[]{:S(2)}, u32[]{:S(2)}) collective-permute-start(bf16[144,256]{1,0:T(8,128)(2,1)S(1)} %get-tuple-element.23.refs_0_), channel_id=1, source_target_pairs={{0,4},{4,0},{8,12},{12,8},{1,5},{5,1},{9,13},{13,9},{2,6},{6,2},{1... | collective-permute-start | bytes 221192 | tf_op jit(solution)/shard_map/ppermute | solution.py:269
  8.2 7.8 %collective-permute-start.1 = (bf16[144,256]{1,0:T(8,128)(2,1)S(1)}, bf16[144,256]{1,0:T(8,128)(2,1)S(1)}, u32[]{:S(2)}, u32[]{:S(2)}) collective-permute-start(bf16[144,256]{1,0:T(8,128)(2,1)S(1)} %get-tuple-element.23.refs_0_), channel_id=1, source_target_pairs={{0,8},{4,12},{8,0},{12,4},{1,9},{5,13},{9,1},{13,5},{2,10},{6,14},... | collective-permute-start | bytes 221192 | tf_op jit(solution)/shard_map/ppermute | solution.py:269
  10.8 6.3 %collective-permute-start.2 = (bf16[144,256]{1,0:T(8,128)(2,1)S(1)}, bf16[144,256]{1,0:T(8,128)(2,1)S(1)}, u32[]{:S(2)}, u32[]{:S(2)}) collective-permute-start(bf16[144,256]{1,0:T(8,128)(2,1)S(1)} %get-tuple-element.23.refs_0_), channel_id=1, source_target_pairs={{0,12},{4,8},{8,4},{12,0},{1,13},{5,9},{9,5},{13,1},{2,14},{6,10},... | collective-permute-start | bytes 221192 | tf_op jit(solution)/shard_map/ppermute | solution.py:269
  10.8 8.0 %collective-permute-start.3 = (bf16[512,256]{1,0:T(8,128)(2,1)S(1)}, bf16[512,256]{1,0:T(8,128)(2,1)S(1)}, u32[]{:S(2)}, u32[]{:S(2)}) collective-permute-start(bf16[512,256]{1,0:T(8,128)(2,1)S(1)} %get-tuple-element.24.refs_4_), channel_id=1, source_target_pairs={{0,16},{16,0},{1,17},{17,1},{2,18},{18,2},{3,19},{19,3},{4,20},{20... | collective-permute-start | bytes 786440 | tf_op jit(solution)/shard_map/ppermute | solution.py:269
  17.1 9.3 %collective-permute-start.4 = (bf16[384,256]{1,0:T(8,128)(2,1)S(1)}, bf16[384,256]{1,0:T(8,128)(2,1)S(1)}, u32[]{:S(2)}, u32[]{:S(2)}) collective-permute-start(bf16[384,256]{1,0:T(8,128)(2,1)S(1)} %pad_maximum_fusion), channel_id=1, source_target_pairs={{0,16},{16,0},{1,17},{17,1},{2,18},{18,2},{3,19},{19,3},{4,20},{20... | collective-permute-start | bytes 589832 | tf_op jit(solution)/shard_map/ppermute | solution.py:269
  20.7 11.3 %collective-permute-start.10 = (bf16[128,256]{1,0:T(8,128)(2,1)S(1)}, bf16[128,256]{1,0:T(8,128)(2,1)S(1)}, u32[]{:S(2)}, u32[]{:S(2)}) collective-permute-start(bf16[128,256]{1,0:T(8,128)(2,1)S(1)} %get-tuple-element.35), channel_id=1, source_target_pairs={{0,12},{4,8},{8,4},{12,0},{1,13},{5,9},{9,5},{13,1},{2,14},{6,10},... | collective-permute-start | bytes 196616 | tf_op jit(solution)/shard_map/ppermute | solution.py:269
  25.8 7.2 %collective-permute-start.8 = (bf16[128,256]{1,0:T(8,128)(2,1)S(1)}, bf16[128,256]{1,0:T(8,128)(2,1)S(1)}, u32[]{:S(2)}, u32[]{:S(2)}) collective-permute-start(bf16[128,256]{1,0:T(8,128)(2,1)S(1)} %get-tuple-element.33), channel_id=1, source_target_pairs={{0,4},{4,0},{8,12},{12,8},{1,5},{5,1},{9,13},{13,9},{2,6},{6,2},{1... | collective-permute-start | bytes 196616 | tf_op jit(solution)/shard_map/ppermute | solution.py:269
  25.8 7.2 %collective-permute-start.9 = (bf16[128,256]{1,0:T(8,128)(2,1)S(1)}, bf16[128,256]{1,0:T(8,128)(2,1)S(1)}, u32[]{:S(2)}, u32[]{:S(2)}) collective-permute-start(bf16[128,256]{1,0:T(8,128)(2,1)S(1)} %get-tuple-element.34), channel_id=1, source_target_pairs={{0,8},{4,12},{8,0},{12,4},{1,9},{5,13},{9,1},{13,5},{2,10},{6,14},... | collective-permute-start | bytes 196616 | tf_op jit(solution)/shard_map/ppermute | solution.py:269
  27.6 5.4 %collective-permute-start.5 = (bf16[128,256]{1,0:T(8,128)(2,1)S(1)}, bf16[128,256]{1,0:T(8,128)(2,1)S(1)}, u32[]{:S(2)}, u32[]{:S(2)}) collective-permute-start(bf16[128,256]{1,0:T(8,128)(2,1)S(1)} %get-tuple-element.30), channel_id=1, source_target_pairs={{0,4},{4,0},{8,12},{12,8},{1,5},{5,1},{9,13},{13,9},{2,6},{6,2},{1... | collective-permute-start | bytes 196616 | tf_op jit(solution)/shard_map/ppermute | solution.py:269
  29.1 5.9 %collective-permute-start.6 = (bf16[128,256]{1,0:T(8,128)(2,1)S(1)}, bf16[128,256]{1,0:T(8,128)(2,1)S(1)}, u32[]{:S(2)}, u32[]{:S(2)}) collective-permute-start(bf16[128,256]{1,0:T(8,128)(2,1)S(1)} %get-tuple-element.31), channel_id=1, source_target_pairs={{0,8},{4,12},{8,0},{12,4},{1,9},{5,13},{9,1},{13,5},{2,10},{6,14},... | collective-permute-start | bytes 196616 | tf_op jit(solution)/shard_map/ppermute | solution.py:269
  32.0 6.1 %collective-permute-start.7 = (bf16[128,256]{1,0:T(8,128)(2,1)S(1)}, bf16[128,256]{1,0:T(8,128)(2,1)S(1)}, u32[]{:S(2)}, u32[]{:S(2)}) collective-permute-start(bf16[128,256]{1,0:T(8,128)(2,1)S(1)} %get-tuple-element.32), channel_id=1, source_target_pairs={{0,12},{4,8},{8,4},{12,0},{1,13},{5,9},{9,5},{13,1},{2,14},{6,10},... | collective-permute-start | bytes 196616 | tf_op jit(solution)/shard_map/ppermute | solution.py:269
  38.9 1.9 %collective-permute-start.11 = (bf16[128,256]{1,0:T(8,128)(2,1)S(1)}, bf16[128,256]{1,0:T(8,128)(2,1)S(1)}, u32[]{:S(2)}, u32[]{:S(2)}) collective-permute-start(bf16[128,256]{1,0:T(8,128)(2,1)S(1)} %get-tuple-element.38), channel_id=1, source_target_pairs={{0,1},{1,0},{2,3},{3,2},{4,5},{5,4},{6,7},{7,6},{8,9},{9,8},{10,11... | collective-permute-start | bytes 196616 | tf_op jit(solution)/shard_map/ppermute | solution.py:269
  38.9 4.5 %collective-permute-start.12 = (bf16[128,256]{1,0:T(8,128)(2,1)S(1)}, bf16[128,256]{1,0:T(8,128)(2,1)S(1)}, u32[]{:S(2)}, u32[]{:S(2)}) collective-permute-start(bf16[128,256]{1,0:T(8,128)(2,1)S(1)} %get-tuple-element.39), channel_id=1, source_target_pairs={{0,2},{1,3},{2,0},{3,1},{4,6},{5,7},{6,4},{7,5},{8,10},{9,11},{10,... | collective-permute-start | bytes 196616 | tf_op jit(solution)/shard_map/ppermute | solution.py:269
  40.5 4.1 %collective-permute-start.13 = (bf16[128,256]{1,0:T(8,128)(2,1)S(1)}, bf16[128,256]{1,0:T(8,128)(2,1)S(1)}, u32[]{:S(2)}, u32[]{:S(2)}) collective-permute-start(bf16[128,256]{1,0:T(8,128)(2,1)S(1)} %get-tuple-element.40), channel_id=1, source_target_pairs={{0,3},{1,2},{2,1},{3,0},{4,7},{5,6},{6,5},{7,4},{8,11},{9,10},{10,... | collective-permute-start | bytes 196616 | tf_op jit(solution)/shard_map/ppermute | solution.py:269

commit v3 on v2

v3 whole, which is shorter than its diff:
```python
import jax
import jax.numpy as jnp
from jax import lax
from jax.experimental import pallas as pl
from jax.experimental.pallas import tpu as pltpu
from jax.sharding import PartitionSpec as P


HEAD_DIM = 128
PAD = 16
F32 = jnp.float32
BF16 = jnp.bfloat16


def silu(v):
    return 0.5 * v * (1.0 + jnp.tanh(0.5 * v))


def dot(a, b):
    return jnp.dot(a, b, preferred_element_type=F32)


def vmem():
    return pl.BlockSpec(memory_space=pltpu.VMEM)


def call(kernel, outs, scratch=(), specs=None, far=()):
    given = {} if specs is None else {"in_specs": specs}
    made = pl.pallas_call(
        kernel,
        out_shape=jax.tree.map(lambda o: pltpu.VMEM(o.shape, o.dtype), outs),
        out_specs=jax.tree.map(lambda _: vmem(), outs),
        scratch_shapes=list(scratch),
        compiler_params=pltpu.CompilerParams(vmem_limit_bytes=16 << 20),
        **given,
    )

    def run(*args):
        spaces = [pltpu.HBM if i in far else pltpu.VMEM for i in range(len(args))]
        args = [pltpu.with_memory_space_constraint(x, space) for x, space in zip(args, spaces)]
        return made(*args)

    return run


def shape(dims, kind=BF16):
    return jax.ShapeDtypeStruct(dims, kind)


def normed_of(table_ref):
    x = table_ref[...].astype(F32)
    center = x - jnp.mean(x, axis=1, keepdims=True)
    return (center * lax.rsqrt(jnp.mean(center * center, axis=1, keepdims=True) + 1e-05)).astype(BF16)


def project_kernel(owner_ref, row_ref, table_hbm, weight_hbm, packet_ref, bulk_ref, weight_ref, table_ref, sems):
    rows, model = table_ref.shape
    kinds, width = weight_ref.shape[1:]
    slots = owner_ref.shape[1]
    lanes = 128 * kinds
    half = model // 2
    first_copy = pltpu.make_async_copy(table_hbm, table_ref, sems.at[0])
    first_copy.start()
    copies = [
        pltpu.make_async_copy(weight_hbm.at[at : at + half], weight_ref.at[at : at + half], sems.at[1 + at // half])
        for at in (0, half)
    ]
    for one in copies:
        one.start()
    packet_ref[rows:, 0:slots] = jnp.broadcast_to(owner_ref[...].astype(F32), (PAD, slots)).astype(BF16)
    packet_ref[rows:, slots : 2 * slots] = jnp.broadcast_to(row_ref[...].astype(F32), (PAD, slots)).astype(BF16)
    spread = (
        lax.broadcasted_iota(jnp.int32, (128, lanes), 1) // kinds
        == lax.broadcasted_iota(jnp.int32, (128, lanes), 0)
    ).astype(F32).astype(BF16)
    kind = lax.broadcasted_iota(jnp.int32, (rows, lanes), 1) % kinds
    masks = [(kind == k).astype(F32).astype(BF16) for k in range(kinds)]
    first_copy.wait()
    normed = normed_of(table_ref)
    start = pl.multiple_of(lax.axis_index("head") * width, width)
    bulk_ref[:, 2 * width :] = table_ref[:, pl.ds(start, width)]
    parts = []
    for at in range(0, model, 128):
        wide = dot(normed[:, at : at + 128], spread).astype(BF16)
        parts.append(jnp.concatenate([wide * mask for mask in masks], axis=0))
    for one in copies:
        one.wait()
    total = dot(jnp.concatenate(parts, axis=1), weight_ref[...].reshape(model * kinds, width))
    gates, values, queries, keys = [silu(total[k * rows : (k + 1) * rows]).astype(BF16) for k in range(kinds)]
    packet_ref[0:rows, :] = queries
    bulk_ref[:, width : 2 * width] = gates
    product = queries.astype(F32) * keys.astype(F32)
    for first in range(0, width, HEAD_DIM):
        cols = slice(first, first + HEAD_DIM)
        score = jnp.sum(product[:, cols], axis=1, keepdims=True)
        bulk_ref[:, cols] = (silu(score * HEAD_DIM ** (-0.5)) * values[:, cols].astype(F32)).astype(BF16)


def one_hot(spot, size):
    lanes = lax.broadcasted_iota(jnp.int32, (spot.shape[0], size), 1).astype(F32)
    return (lanes == spot).astype(F32).astype(BF16)


def loop(size, body):
    if size <= 4:
        for j in range(size):
            body(j)
    else:
        lax.fori_loop(0, size, lambda j, c: (body(j), c)[1], 0)


def sort_kernel(users, ctx_size, held, *refs):
    packets, joined_ref, bulks = refs[:ctx_size], refs[ctx_size], refs[ctx_size + 1 : ctx_size + 1 + users]
    outs = refs[ctx_size + 1 + users :]
    sends = outs[: ctx_size - 1]
    extra_ref, query_ref, spot_ref, id_ref = outs[ctx_size - 1 :]
    me_user = lax.axis_index("users")
    me_ctx = lax.axis_index("ctx")
    rows = bulks[0].shape[0]
    count, width = query_ref.shape
    slots = count // ctx_size
    owners = [
        [((me_user ^ k) * ctx_size + (me_ctx ^ m)).astype(F32) for m in range(ctx_size)] for k in range(users)
    ]
    for m in range(ctx_size):
        id_ref[m] = jnp.transpose(packets[m][rows:, :].astype(F32))
    lane = lax.broadcasted_iota(jnp.int32, (slots, 128), 1)

    def find(j):
        owner = id_ref[j, 0:slots, 0:1]
        row = id_ref[j, slots : 2 * slots, 0:1]
        spots = jnp.full((slots, 128), -1.0, F32)
        group = jnp.full((slots, 1), -1.0, F32)
        for k in range(users):
            spot = jnp.full((slots, 1), -1.0, F32)
            for m in range(ctx_size):
                spot = jnp.where(owner == owners[k][m], row + float(m * rows), spot)
            spots = jnp.where(lane == k, spot, spots)
            group = jnp.where(owner == owners[k][0], row + float(k * rows), group)
        first = j * slots if isinstance(j, int) else pl.multiple_of(j * slots, slots)
        spot_ref[pl.ds(first, slots), :] = jnp.where(lane == users, group, spots)

    loop(ctx_size, find)
    block = min(count, 512)
    both = jnp.concatenate([bulk[...] for bulk in bulks], axis=0)

    def gather(b):
        first = b * block if isinstance(b, int) else pl.multiple_of(b * block, block)
        group = spot_ref[pl.ds(first, block), users : users + 1]
        extra_ref[pl.ds(first, block), :] = dot(one_hot(group, users * rows), both).astype(BF16)
        spot = spot_ref[pl.ds(first, block), 0:1]
        query_ref[pl.ds(first, block), :] = dot(one_hot(spot, ctx_size * rows), joined_ref[...]).astype(BF16)

    loop(count // block, gather)
    before = (
        lax.broadcasted_iota(jnp.int32, (slots, slots), 0) < lax.broadcasted_iota(jnp.int32, (slots, slots), 1)
    ).astype(F32).astype(BF16)
    for j in range(1, ctx_size):
        line = packets[j][rows:, 0:slots].astype(F32)
        inside = jnp.zeros(line.shape, jnp.bool_)
        for k in range(users):
            inside = inside | (line == owners[k][0])
        rank = jnp.where(inside, dot(inside.astype(F32).astype(BF16), before), -1.0)[0:1, :]
        keep = lax.broadcasted_iota(jnp.int32, (held, slots), 0).astype(F32) == rank
        sends[j - 1][...] = dot(
            keep.astype(F32).astype(BF16), extra_ref[j * slots : (j + 1) * slots, width:]
        ).astype(BF16)


def attend_kernel(users, ctx_size, history, *refs):
    spot_ref, part_ref, extra_ref, key_ref, value_ref = refs[:5]
    relays = refs[5 : 4 + users]
    outs, sum_ref = refs[4 + users : -1], refs[-1]
    count, width = part_ref.shape
    slots = count // ctx_size
    block = min(count, 512)

    def attend(b):
        first = b * block if isinstance(b, int) else pl.multiple_of(b * block, block)
        queries = part_ref[pl.ds(first, block), :].astype(F32)
        for k in range(1, users):
            spot = spot_ref[pl.ds(first, block), k : k + 1]
            queries = queries + dot(one_hot(spot, relays[k - 1].shape[0]), relays[k - 1][...])
        queries = queries.astype(BF16)
        for at in range(0, width, HEAD_DIM):
            cols = slice(at, at + HEAD_DIM)
            scores = lax.dot_general(
                queries[:, cols], key_ref[:, cols], (((1,), (1,)), ((), ())), preferred_element_type=F32
            ) * (0.5 * HEAD_DIM ** (-0.5))
            weights = (scores + scores * jnp.tanh(scores)).astype(BF16)
            sum_ref[pl.ds(first, block), cols] = dot(weights, value_ref[:, cols])

    loop(count // block, attend)
    for j in range(ctx_size):
        span = slice(j * slots, (j + 1) * slots)
        outs[j][...] = (sum_ref[span, :] * history ** (-0.5) + extra_ref[span, 0:width].astype(F32)).astype(BF16)


def mix_kernel(users, ctx_size, head_size, held, *refs):
    owner_ref, extra_ref, weight_ref = refs[:3]
    sums = refs[3 : 3 + ctx_size]
    packs = refs[3 + ctx_size : 2 + 2 * ctx_size]
    outs = refs[2 + 2 * ctx_size : 2 + 2 * ctx_size + head_size]
    residual_ref = refs[2 + 2 * ctx_size + head_size]
    me_user = lax.axis_index("users")
    me_ctx = lax.axis_index("ctx")
    me_head = lax.axis_index("head")
    slots, width = residual_ref.shape
    owner = jnp.transpose(jnp.broadcast_to(owner_ref[...].astype(F32), (8, slots)))[:, 0:1]
    lanes = 128
    lane = lax.broadcasted_iota(jnp.int32, (slots, lanes), 1)
    inside = jnp.zeros((slots, lanes), jnp.bool_)
    for k in range(users):
        named = (me_user ^ k) * ctx_size + (me_ctx ^ lane)
        inside = inside | ((owner == named.astype(F32)) & (lane < ctx_size))
    after = (
        lax.broadcasted_iota(jnp.int32, (slots, slots), 1) < lax.broadcasted_iota(jnp.int32, (slots, slots), 0)
    ).astype(F32).astype(BF16)
    rank = jnp.where(inside, dot(after, inside.astype(F32).astype(BF16)), -1.0)
    attended = sums[0][...].astype(F32)
    for m in range(1, ctx_size):
        attended = attended + sums[m][...].astype(F32)
    both = extra_ref[0:slots, width:].astype(F32)
    if ctx_size > 1:
        spots = lax.broadcasted_iota(jnp.int32, (slots, (ctx_size - 1) * held), 1).astype(F32)
        spot = jnp.full((slots, 1), -1.0, F32)
        for m in range(1, ctx_size):
            mine = rank[:, m : m + 1]
            spot = jnp.where(mine >= 0.0, mine + float((m - 1) * held), spot)
        both = both + dot(
            (spots == spot).astype(F32).astype(BF16), jnp.concatenate([pack[...] for pack in packs], axis=0)
        )
    gates, residual = both[:, 0:width], both[:, width:]
    residual_ref[...] = residual.astype(BF16)
    parts = []
    for at in range(0, width, HEAD_DIM):
        one = attended[:, at : at + HEAD_DIM]
        center = one - jnp.mean(one, axis=1, keepdims=True)
        parts.append(
            center
            * lax.rsqrt(jnp.mean(center * center, axis=1, keepdims=True) + 1e-05)
            * gates[:, at : at + HEAD_DIM]
        )
    hidden = jnp.concatenate(parts, axis=1).astype(BF16)
    for t in range(head_size):
        first = pl.multiple_of((me_head ^ t) * width, width)
        outs[t][...] = dot(hidden, weight_ref[:, pl.ds(first, width)]).astype(outs[t].dtype)


def swap(x, axis, k):
    return lax.ppermute(x, axis, [(i, i ^ k) for i in range(lax.axis_size(axis))])


def layer(
    counts, cand_owner, cand_row, item_table, proj_weight, out_weight, key_cache, value_cache
):
    users = lax.axis_size("users")
    ctx_size = lax.axis_size("ctx")
    head_size = lax.axis_size("head")
    slots = cand_row.shape[1]
    rows, model = item_table.shape
    width = proj_weight.shape[2]
    span = rows + PAD
    history = key_cache.shape[1] * ctx_size
    capacity = max(2, 2 * slots // (users * ctx_size))
    held = max(PAD, -(-users * min(capacity, slots) // PAD) * PAD)
    owner = cand_owner.reshape(1, slots)
    kinds = proj_weight.shape[1]
    hbm = pl.BlockSpec(memory_space=pl.ANY)
    packet, bulk = call(
        project_kernel,
        (shape((span, width)), shape((rows, 3 * width))),
        (
            pltpu.VMEM((model, kinds, width), BF16),
            pltpu.VMEM((rows, model), BF16),
            pltpu.SemaphoreType.DMA((3,)),
        ),
        specs=[vmem()] * 2 + [hbm] * 2,
        far=(0, 1, 2, 3),
    )(owner, cand_row, item_table, proj_weight)
    packets = [packet] + [swap(packet, "ctx", m) for m in range(1, ctx_size)]
    bulks = [bulk] + [swap(bulk, "users", k) for k in range(1, users)]
    joined = jnp.concatenate([one[0:rows] for one in packets], axis=0)
    relays = [swap(joined, "users", k) for k in range(1, users)]
    count = ctx_size * slots
    *packs, extra, part, spots = call(
        lambda *refs: sort_kernel(users, ctx_size, held, *refs),
        (shape((held, 2 * width)),) * (ctx_size - 1)
        + (shape((count, 3 * width)), shape((count, width)), shape((count, 128), F32)),
        (pltpu.VMEM((ctx_size, width, PAD), F32),),
    )(*packets, joined, *bulks)
    packs = [swap(packs[m - 1], "ctx", m) for m in range(1, ctx_size)]
    sums = call(
        lambda *refs: attend_kernel(users, ctx_size, history, *refs),
        (shape((slots, width)),) * ctx_size,
        (pltpu.VMEM((count, width), F32),),
    )(spots, part, extra, key_cache[0], value_cache[0], *relays)
    sums = [sums[0]] + [swap(sums[m], "ctx", m) for m in range(1, ctx_size)]
    *parts, residual = call(
        lambda *refs: mix_kernel(users, ctx_size, head_size, held, *refs),
        (shape((slots, width), F32),) + (shape((slots, width)),) * (head_size - 1) + (shape((slots, width)),),
    )(owner, extra, out_weight, *sums, *packs)
    got = [parts[0]] + [swap(parts[t], "head", t) for t in range(1, head_size)]
    total = residual.astype(F32)
    for one in got:
        total = total + one.astype(F32)
    slot = lax.broadcasted_iota(jnp.int32, total.shape, 0)
    return jnp.where(slot < counts[0] - lax.axis_index("ctx") * slots, total, 0.0).astype(BF16)[None]


def solution(mesh):
    return jax.shard_map(
        layer,
        mesh=mesh,
        in_specs=(
            P("users"),
            P("users", "ctx", None),
            P("users", "ctx"),
            P(("users", "ctx"), None),
            P(None, None, "head"),
            P("head", None),
            P("users", "ctx", "head"),
            P("users", "ctx", "head"),
        ),
        out_specs=P("users", "ctx", "head"),
        check_vma=False,
    )
```

time: 45.5 us -> 48.9 us (1.075)
  waiting for transfers between devices: 13.6 us -> 21.5 us
  starting transfers between devices: 21.3 us -> 18.6 us
  Pallas kernels: 8.93 us -> 7.08 us
    ppermute x14, waiting for transfers between devices: 13.6 us -> 21.5 us  [swap(): lax.ppermute(x, axis, [(i, i ^ k) for i in range(lax.axis_size(axis))])]
    ppermute x14, starting transfers between devices: 21.3 us -> 18.6 us  [swap(): lax.ppermute(x, axis, [(i, i ^ k) for i in range(lax.axis_size(axis))])]
    pallas_call x4, Pallas kernels: 8.93 us -> 7.08 us  [run(): return made(*args)]
  transfers between devices with their start and end apart: 14 -> 14, of which waited for: 7 -> 9; matrix products, arithmetic and copies ran while one was open for 0% -> 0% of each run, Pallas kernels for 7% -> 5%
where the time goes in v3:
time: 48.9 us; the launch traced here: 48.7 us
  waiting for transfers between devices  21.5 us (44%)
  starting transfers between devices  18.6 us (38%)
  Pallas kernels  7.08 us (14%)
  between operations  0.76 us (2%)
  other arithmetic  0.74 us (2%)
    ppermute x14, waiting for transfers between devices, swap(): lax.ppermute(x, axis, [(i, i ^ k) for i in range(lax.axis_size(axis))])  21.5 us
    ppermute x14, starting transfers between devices, swap(): lax.ppermute(x, axis, [(i, i ^ k) for i in range(lax.axis_size(axis))])  18.6 us
    pallas_call x4, Pallas kernels, run(): return made(*args)  7.08 us
  transfers between devices with their start and end apart: 14, of which 9 were waited for; matrix products, arithmetic and copies ran while one was open for 0% of the time, Pallas kernels for 5%

profile of v3, /device:TPU:0, one launch (start us, length us, event | category | flops | bytes accessed | tf_op | source)
XLA Modules:
  0.0 48.7 jit_solution(6368373238380676083)
XLA Ops:
  0.0 0.0 copy-start.1
  0.0 0.0 copy-start.2
  0.0 3.7 %shard_map.82 = (bf16[144,256]{1,0:T(8,128)(2,1)S(1)}, bf16[128,768]{1,0:T(8,128)(2,1)S(1)}) custom-call(s32[1,128]{1,0:T(1,128)} %bitcast.9, s32[1,128]{1,0:T(1,128)} %row_ref.1, bf16[128,1024]{1,0:T(8,128)(2,1)} %table_hbm.1, bf16[1024,4,256]{2,1,0:T(4,128)(2,1)} %weight_hbm.1), custom_call_target="tpu_custom_call" | custom-call | tf_op jit(solution)/shard_map/pallas_call | solution.py:41
  3.8 0.0 copy-start
  3.8 0.0 copy-start.3
  3.8 3.1 %collective-permute-start = (bf16[144,256]{1,0:T(8,128)(2,1)S(1)}, bf16[144,256]{1,0:T(8,128)(2,1)S(1)}, u32[]{:S(2)}, u32[]{:S(2)}) collective-permute-start(bf16[144,256]{1,0:T(8,128)(2,1)S(1)} %get-tuple-element.22.refs_0_), channel_id=1, source_target_pairs={{0,4},{4,0},{8,12},{12,8},{1,5},{5,1},{9,13},{13,9},{2,6},{6,2},{1... | collective-permute-start | bytes 221192 | tf_op jit(solution)/shard_map/ppermute | solution.py:251
  6.9 2.6 %collective-permute-start.1 = (bf16[144,256]{1,0:T(8,128)(2,1)S(1)}, bf16[144,256]{1,0:T(8,128)(2,1)S(1)}, u32[]{:S(2)}, u32[]{:S(2)}) collective-permute-start(bf16[144,256]{1,0:T(8,128)(2,1)S(1)} %get-tuple-element.22.refs_0_), channel_id=1, source_target_pairs={{0,8},{4,12},{8,0},{12,4},{1,9},{5,13},{9,1},{13,5},{2,10},{6,14},... | collective-permute-start | bytes 221192 | tf_op jit(solution)/shard_map/ppermute | solution.py:251
  9.5 0.0 collective-permute-start.2
  9.5 0.0 collective-permute-done.refs_1_
  9.5 5.2 %collective-permute-done.1.refs_2_ = bf16[144,256]{1,0:T(8,128)(2,1)S(1)} collective-permute-done((bf16[144,256]{1,0:T(8,128)(2,1)S(1)}, bf16[144,256]{1,0:T(8,128)(2,1)S(1)}, u32[]{:S(2)}, u32[]{:S(2)}) %collective-permute-start.1) | collective-permute-done | bytes 73760 | tf_op jit(solution)/shard_map/ppermute | solution.py:251
  14.7 1.0 %collective-permute-done.2.refs_3_ = bf16[144,256]{1,0:T(8,128)(2,1)S(1)} collective-permute-done((bf16[144,256]{1,0:T(8,128)(2,1)S(1)}, bf16[144,256]{1,0:T(8,128)(2,1)S(1)}, u32[]{:S(2)}, u32[]{:S(2)}) %collective-permute-start.2) | collective-permute-done | bytes 73760 | tf_op jit(solution)/shard_map/ppermute | solution.py:251
  15.8 1.6 %collective-permute-start.4 = (bf16[512,256]{1,0:T(8,128)(2,1)S(1)}, bf16[512,256]{1,0:T(8,128)(2,1)S(1)}, u32[]{:S(2)}, u32[]{:S(2)}) collective-permute-start(bf16[512,256]{1,0:T(8,128)(2,1)S(1)} %pad_maximum_fusion.refs_4_), channel_id=1, source_target_pairs={{0,16},{16,0},{1,17},{17,1},{2,18},{18,2},{3,19},{19,3},{4,20},{20... | collective-permute-start | bytes 786440 | tf_op jit(solution)/shard_map/ppermute | solution.py:251
  17.3 0.5 %collective-permute-start.3 = (bf16[128,768]{1,0:T(8,128)(2,1)S(1)}, bf16[128,768]{1,0:T(8,128)(2,1)S(1)}, u32[]{:S(2)}, u32[]{:S(2)}) collective-permute-start(bf16[128,768]{1,0:T(8,128)(2,1)S(1)} %get-tuple-element.23.refs_5_), channel_id=1, source_target_pairs={{0,16},{16,0},{1,17},{17,1},{2,18},{18,2},{3,19},{19,3},{4,20},{20... | collective-permute-start | bytes 589832 | tf_op jit(solution)/shard_map/ppermute | solution.py:251
  17.9 8.4 %collective-permute-done.3.refs_6_ = bf16[128,768]{1,0:T(8,128)(2,1)S(1)} collective-permute-done((bf16[128,768]{1,0:T(8,128)(2,1)S(1)}, bf16[128,768]{1,0:T(8,128)(2,1)S(1)}, u32[]{:S(2)}, u32[]{:S(2)}) %collective-permute-start.3) | collective-permute-done | bytes 196640 | tf_op jit(solution)/shard_map/ppermute | solution.py:251
  26.3 1.5 %shard_map.83 = (bf16[64,512]{1,0:T(8,128)(2,1)S(1)}, bf16[64,512]{1,0:T(8,128)(2,1)S(1)}, bf16[64,512]{1,0:T(8,128)(2,1)S(1)}, bf16[512,768]{1,0:T(8,128)(2,1)S...) custom-call(bf16[144,256]{1,0:T(8,128)(2,1)S(1)} %get-tuple-element.22.refs_0_, ...), custom_call_target="tpu_custom_call" | custom-call | tf_op jit(solution)/shard_map/pallas_call | solution.py:41
  27.8 1.4 %collective-permute-start.10 = (bf16[64,512]{1,0:T(8,128)(2,1)S(1)}, bf16[64,512]{1,0:T(8,128)(2,1)S(1)}, u32[]{:S(2)}, u32[]{:S(2)}) collective-permute-start(bf16[64,512]{1,0:T(8,128)(2,1)S(1)} %get-tuple-element.33), channel_id=1, source_target_pairs={{0,12},{4,8},{8,4},{12,0},{1,13},{5,9},{9,5},{13,1},{2,14},{6,10},... | collective-permute-start | bytes 196616 | tf_op jit(solution)/shard_map/ppermute | solution.py:251
  29.2 2.0 %collective-permute-start.8 = (bf16[64,512]{1,0:T(8,128)(2,1)S(1)}, bf16[64,512]{1,0:T(8,128)(2,1)S(1)}, u32[]{:S(2)}, u32[]{:S(2)}) collective-permute-start(bf16[64,512]{1,0:T(8,128)(2,1)S(1)} %get-tuple-element.31), channel_id=1, source_target_pairs={{0,4},{4,0},{8,12},{12,8},{1,5},{5,1},{9,13},{13,9},{2,6},{6,2},{1... | collective-permute-start | bytes 196616 | tf_op jit(solution)/shard_map/ppermute | solution.py:251
  31.2 1.0 %collective-permute-start.9 = (bf16[64,512]{1,0:T(8,128)(2,1)S(1)}, bf16[64,512]{1,0:T(8,128)(2,1)S(1)}, u32[]{:S(2)}, u32[]{:S(2)}) collective-permute-start(bf16[64,512]{1,0:T(8,128)(2,1)S(1)} %get-tuple-element.32), channel_id=1, source_target_pairs={{0,8},{4,12},{8,0},{12,4},{1,9},{5,13},{9,1},{13,5},{2,10},{6,14},... | collective-permute-start | bytes 196616 | tf_op jit(solution)/shard_map/ppermute | solution.py:251
  32.2 0.0 collective-permute-done.4.refs_5_
  32.2 0.0 copy-done.1
  32.2 0.0 copy-done.2
  32.2 1.0 %shard_map.84 = (bf16[128,256]{1,0:T(8,128)(2,1)S(1)}, bf16[128,256]{1,0:T(8,128)(2,1)S(1)}, bf16[128,256]{1,0:T(8,128)(2,1)S(1)}, bf16[128,256]{1,0:T(8,128)(2,1)S(1)}) custom-call(f32[512,128]{1,0:T(8,128)S(1)} %get-tuple-element.25.refs_0_, bf16[512,256]{1,0:T(8,128)(2,1)S(1)} %get-tuple-element.26.refs_1_, ...), custom_call_target="tpu_custom_call" | custom-call | tf_op jit(solution)/shard_map/pallas_call | solution.py:41
  33.2 0.6 %collective-permute-start.5 = (bf16[128,256]{1,0:T(8,128)(2,1)S(1)}, bf16[128,256]{1,0:T(8,128)(2,1)S(1)}, u32[]{:S(2)}, u32[]{:S(2)}) collective-permute-start(bf16[128,256]{1,0:T(8,128)(2,1)S(1)} %get-tuple-element.28), channel_id=1, source_target_pairs={{0,4},{4,0},{8,12},{12,8},{1,5},{5,1},{9,13},{13,9},{2,6},{6,2},{1... | collective-permute-start | bytes 196616 | tf_op jit(solution)/shard_map/ppermute | solution.py:251
  33.8 1.5 %collective-permute-start.6 = (bf16[128,256]{1,0:T(8,128)(2,1)S(1)}, bf16[128,256]{1,0:T(8,128)(2,1)S(1)}, u32[]{:S(2)}, u32[]{:S(2)}) collective-permute-start(bf16[128,256]{1,0:T(8,128)(2,1)S(1)} %get-tuple-element.29), channel_id=1, source_target_pairs={{0,8},{4,12},{8,0},{12,4},{1,9},{5,13},{9,1},{13,5},{2,10},{6,14},... | collective-permute-start | bytes 196616 | tf_op jit(solution)/shard_map/ppermute | solution.py:251
  35.3 0.0 collective-permute-done.10.refs_9_
  35.3 2.4 %collective-permute-start.7 = (bf16[128,256]{1,0:T(8,128)(2,1)S(1)}, bf16[128,256]{1,0:T(8,128)(2,1)S(1)}, u32[]{:S(2)}, u32[]{:S(2)}) collective-permute-start(bf16[128,256]{1,0:T(8,128)(2,1)S(1)} %get-tuple-element.30), channel_id=1, source_target_pairs={{0,12},{4,8},{8,4},{12,0},{1,13},{5,9},{9,5},{13,1},{2,14},{6,10},... | collective-permute-start | bytes 196616 | tf_op jit(solution)/shard_map/ppermute | solution.py:251
  38.4 0.0 collective-permute-done.8.refs_7_
  38.4 0.4 collective-permute-done.9.refs_8_
  38.8 0.6 %collective-permute-done.5.refs_4_ = bf16[128,256]{1,0:T(8,128)(2,1)S(1)} collective-permute-done((bf16[128,256]{1,0:T(8,128)(2,1)S(1)}, bf16[128,256]{1,0:T(8,128)(2,1)S(1)}, u32[]{:S(2)}, u32[]{:S(2)}) %collective-permute-start.5) | collective-permute-done | bytes 65568 | tf_op jit(solution)/shard_map/ppermute | solution.py:251
  39.4 0.8 %collective-permute-done.6.refs_5_ = bf16[128,256]{1,0:T(8,128)(2,1)S(1)} collective-permute-done((bf16[128,256]{1,0:T(8,128)(2,1)S(1)}, bf16[128,256]{1,0:T(8,128)(2,1)S(1)}, u32[]{:S(2)}, u32[]{:S(2)}) %collective-permute-start.6) | collective-permute-done | bytes 65568 | tf_op jit(solution)/shard_map/ppermute | solution.py:251
  40.2 1.2 %collective-permute-done.7.refs_6_ = bf16[128,256]{1,0:T(8,128)(2,1)S(1)} collective-permute-done((bf16[128,256]{1,0:T(8,128)(2,1)S(1)}, bf16[128,256]{1,0:T(8,128)(2,1)S(1)}, u32[]{:S(2)}, u32[]{:S(2)}) %collective-permute-start.7) | collective-permute-done | bytes 65568 | tf_op jit(solution)/shard_map/ppermute | solution.py:251
  41.4 0.0 copy-done
  41.4 0.0 copy-done.3
  41.4 0.9 %shard_map.85 = (f32[128,256]{1,0:T(8,128)S(1)}, bf16[128,256]{1,0:T(8,128)(2,1)S(1)}, bf16[128,256]{1,0:T(8,128)(2,1)S(1)}, bf16[128,256]{1,0:T(8,128)(2,1)S(1)}, bf16[128,256]{1,0:T(8,128)(2,1)S(1)}) custom-call(s32[1,128]{1,0:T(1,128)S(1)} %bitcast.10, bf16[512,768]{1,0:T(8,128)(2,1)S(1)} %get-tuple-element.24.refs_2_.refs_1_, ...), custom_call_target="tpu_custom_call" | custom-call | tf_op jit(solution)/shard_map/pallas_call | solution.py:41
  42.3 0.1 collective-permute-start.11
  42.4 1.6 %collective-permute-start.12 = (bf16[128,256]{1,0:T(8,128)(2,1)S(1)}, bf16[128,256]{1,0:T(8,128)(2,1)S(1)}, u32[]{:S(2)}, u32[]{:S(2)}) collective-permute-start(bf16[128,256]{1,0:T(8,128)(2,1)S(1)} %get-tuple-element.37), channel_id=1, source_target_pairs={{0,2},{1,3},{2,0},{3,1},{4,6},{5,7},{6,4},{7,5},{8,10},{9,11},{10,... | collective-permute-start | bytes 196616 | tf_op jit(solution)/shard_map/ppermute | solution.py:251
  44.0 0.3 collective-permute-start.13
  44.2 0.0 collective-permute-done.11
  44.2 2.6 %collective-permute-done.12 = bf16[128,256]{1,0:T(8,128)(2,1)S(1)} collective-permute-done((bf16[128,256]{1,0:T(8,128)(2,1)S(1)}, bf16[128,256]{1,0:T(8,128)(2,1)S(1)}, u32[]{:S(2)}, u32[]{:S(2)}) %collective-permute-start.12) | collective-permute-done | bytes 65568 | tf_op jit(solution)/shard_map/ppermute | solution.py:251
  46.9 1.1 %collective-permute-done.13 = bf16[128,256]{1,0:T(8,128)(2,1)S(1)} collective-permute-done((bf16[128,256]{1,0:T(8,128)(2,1)S(1)}, bf16[128,256]{1,0:T(8,128)(2,1)S(1)}, u32[]{:S(2)}, u32[]{:S(2)}) %collective-permute-start.13) | collective-permute-done | bytes 65568 | tf_op jit(solution)/shard_map/ppermute | solution.py:251
  48.0 0.7 %fusion = bf16[1,128,256]{2,1,0:T(8,128)(2,1)} fusion(bf16[128,256]{1,0:T(8,128)(2,1)S(1)} %collective-permute-done.13, bf16[128,256]{1,0:T(8,128)(2,1)S(1)} %collective-permute-done.12, bf16[128,256]{1,0:T(8,128)(2,1)S(1)} %collective-permute-done.11, f32[128,256]{1,0:T(8,128)S(1)} %get-tuple-element.35, bf16[128,256]{1,0:T(8,128)(2,1)S(1)} %get-tuple-element.34, ...), kind=kLoop, calls=%fused_computation.2 | loop fusion | flops 327680 | bytes 458880 | tf_op jit(solution)/shard_map/broadcast_in_dim | solution.py:308
  (6 shorter events, 0.0 us)
Async XLA Ops:
  0.0 32.2 %copy-start.1 = (bf16[1,512,256]{2,1,0:T(8,128)(2,1)S(1)}, bf16[1,512,256]{2,1,0:T(8,128)(2,1)}, u32[]{:S(2)}) copy-start(bf16[1,512,256]{2,1,0:T(8,128)(2,1)} %param.14) | copy-start | bytes 786436
  0.0 32.2 %copy-start.2 = (bf16[1,512,256]{2,1,0:T(8,128)(2,1)S(1)}, bf16[1,512,256]{2,1,0:T(8,128)(2,1)}, u32[]{:S(2)}) copy-start(bf16[1,512,256]{2,1,0:T(8,128)(2,1)} %param.15) | copy-start | bytes 786436
  3.8 37.7 %copy-start = (bf16[256,1024]{1,0:T(8,128)(2,1)S(1)}, bf16[256,1024]{1,0:T(8,128)(2,1)}, u32[]{:S(2)}) copy-start(bf16[256,1024]{1,0:T(8,128)(2,1)} %refs_2_.1) | copy-start | bytes 1572868
  3.8 37.7 %copy-start.3 = (s32[1,128,1]{1,2,0:T(1,128)S(1)}, s32[1,128,1]{1,2,0:T(1,128)}, u32[]{:S(2)}) copy-start(s32[1,128,1]{1,2,0:T(1,128)} %param.9) | copy-start | bytes 1540
  3.8 5.7 %collective-permute-start = (bf16[144,256]{1,0:T(8,128)(2,1)S(1)}, bf16[144,256]{1,0:T(8,128)(2,1)S(1)}, u32[]{:S(2)}, u32[]{:S(2)}) collective-permute-start(bf16[144,256]{1,0:T(8,128)(2,1)S(1)} %get-tuple-element.22.refs_0_), channel_id=1, source_target_pairs={{0,4},{4,0},{8,12},{12,8},{1,5},{5,1},{9,13},{13,9},{2,6},{6,2},{1... | collective-permute-start | bytes 221192 | tf_op jit(solution)/shard_map/ppermute | solution.py:251
  6.9 7.8 %collective-permute-start.1 = (bf16[144,256]{1,0:T(8,128)(2,1)S(1)}, bf16[144,256]{1,0:T(8,128)(2,1)S(1)}, u32[]{:S(2)}, u32[]{:S(2)}) collective-permute-start(bf16[144,256]{1,0:T(8,128)(2,1)S(1)} %get-tuple-element.22.refs_0_), channel_id=1, source_target_pairs={{0,8},{4,12},{8,0},{12,4},{1,9},{5,13},{9,1},{13,5},{2,10},{6,14},... | collective-permute-start | bytes 221192 | tf_op jit(solution)/shard_map/ppermute | solution.py:251
  9.5 6.3 %collective-permute-start.2 = (bf16[144,256]{1,0:T(8,128)(2,1)S(1)}, bf16[144,256]{1,0:T(8,128)(2,1)S(1)}, u32[]{:S(2)}, u32[]{:S(2)}) collective-permute-start(bf16[144,256]{1,0:T(8,128)(2,1)S(1)} %get-tuple-element.22.refs_0_), channel_id=1, source_target_pairs={{0,12},{4,8},{8,4},{12,0},{1,13},{5,9},{9,5},{13,1},{2,14},{6,10},... | collective-permute-start | bytes 221192 | tf_op jit(solution)/shard_map/ppermute | solution.py:251
  15.8 16.5 %collective-permute-start.4 = (bf16[512,256]{1,0:T(8,128)(2,1)S(1)}, bf16[512,256]{1,0:T(8,128)(2,1)S(1)}, u32[]{:S(2)}, u32[]{:S(2)}) collective-permute-start(bf16[512,256]{1,0:T(8,128)(2,1)S(1)} %pad_maximum_fusion.refs_4_), channel_id=1, source_target_pairs={{0,16},{16,0},{1,17},{17,1},{2,18},{18,2},{3,19},{19,3},{4,20},{20... | collective-permute-start | bytes 786440 | tf_op jit(solution)/shard_map/ppermute | solution.py:251
  17.3 9.0 %collective-permute-start.3 = (bf16[128,768]{1,0:T(8,128)(2,1)S(1)}, bf16[128,768]{1,0:T(8,128)(2,1)S(1)}, u32[]{:S(2)}, u32[]{:S(2)}) collective-permute-start(bf16[128,768]{1,0:T(8,128)(2,1)S(1)} %get-tuple-element.23.refs_5_), channel_id=1, source_target_pairs={{0,16},{16,0},{1,17},{17,1},{2,18},{18,2},{3,19},{19,3},{4,20},{20... | collective-permute-start | bytes 589832 | tf_op jit(solution)/shard_map/ppermute | solution.py:251
  27.8 7.5 %collective-permute-start.10 = (bf16[64,512]{1,0:T(8,128)(2,1)S(1)}, bf16[64,512]{1,0:T(8,128)(2,1)S(1)}, u32[]{:S(2)}, u32[]{:S(2)}) collective-permute-start(bf16[64,512]{1,0:T(8,128)(2,1)S(1)} %get-tuple-element.33), channel_id=1, source_target_pairs={{0,12},{4,8},{8,4},{12,0},{1,13},{5,9},{9,5},{13,1},{2,14},{6,10},... | collective-permute-start | bytes 196616 | tf_op jit(solution)/shard_map/ppermute | solution.py:251
  29.2 9.2 %collective-permute-start.8 = (bf16[64,512]{1,0:T(8,128)(2,1)S(1)}, bf16[64,512]{1,0:T(8,128)(2,1)S(1)}, u32[]{:S(2)}, u32[]{:S(2)}) collective-permute-start(bf16[64,512]{1,0:T(8,128)(2,1)S(1)} %get-tuple-element.31), channel_id=1, source_target_pairs={{0,4},{4,0},{8,12},{12,8},{1,5},{5,1},{9,13},{13,9},{2,6},{6,2},{1... | collective-permute-start | bytes 196616 | tf_op jit(solution)/shard_map/ppermute | solution.py:251
  31.2 7.6 %collective-permute-start.9 = (bf16[64,512]{1,0:T(8,128)(2,1)S(1)}, bf16[64,512]{1,0:T(8,128)(2,1)S(1)}, u32[]{:S(2)}, u32[]{:S(2)}) collective-permute-start(bf16[64,512]{1,0:T(8,128)(2,1)S(1)} %get-tuple-element.32), channel_id=1, source_target_pairs={{0,8},{4,12},{8,0},{12,4},{1,9},{5,13},{9,1},{13,5},{2,10},{6,14},... | collective-permute-start | bytes 196616 | tf_op jit(solution)/shard_map/ppermute | solution.py:251
  33.2 6.1 %collective-permute-start.5 = (bf16[128,256]{1,0:T(8,128)(2,1)S(1)}, bf16[128,256]{1,0:T(8,128)(2,1)S(1)}, u32[]{:S(2)}, u32[]{:S(2)}) collective-permute-start(bf16[128,256]{1,0:T(8,128)(2,1)S(1)} %get-tuple-element.28), channel_id=1, source_target_pairs={{0,4},{4,0},{8,12},{12,8},{1,5},{5,1},{9,13},{13,9},{2,6},{6,2},{1... | collective-permute-start | bytes 196616 | tf_op jit(solution)/shard_map/ppermute | solution.py:251
  33.8 6.4 %collective-permute-start.6 = (bf16[128,256]{1,0:T(8,128)(2,1)S(1)}, bf16[128,256]{1,0:T(8,128)(2,1)S(1)}, u32[]{:S(2)}, u32[]{:S(2)}) collective-permute-start(bf16[128,256]{1,0:T(8,128)(2,1)S(1)} %get-tuple-element.29), channel_id=1, source_target_pairs={{0,8},{4,12},{8,0},{12,4},{1,9},{5,13},{9,1},{13,5},{2,10},{6,14},... | collective-permute-start | bytes 196616 | tf_op jit(solution)/shard_map/ppermute | solution.py:251
  35.3 6.2 %collective-permute-start.7 = (bf16[128,256]{1,0:T(8,128)(2,1)S(1)}, bf16[128,256]{1,0:T(8,128)(2,1)S(1)}, u32[]{:S(2)}, u32[]{:S(2)}) collective-permute-start(bf16[128,256]{1,0:T(8,128)(2,1)S(1)} %get-tuple-element.30), channel_id=1, source_target_pairs={{0,12},{4,8},{8,4},{12,0},{1,13},{5,9},{9,5},{13,1},{2,14},{6,10},... | collective-permute-start | bytes 196616 | tf_op jit(solution)/shard_map/ppermute | solution.py:251
  42.3 1.9 %collective-permute-start.11 = (bf16[128,256]{1,0:T(8,128)(2,1)S(1)}, bf16[128,256]{1,0:T(8,128)(2,1)S(1)}, u32[]{:S(2)}, u32[]{:S(2)}) collective-permute-start(bf16[128,256]{1,0:T(8,128)(2,1)S(1)} %get-tuple-element.36), channel_id=1, source_target_pairs={{0,1},{1,0},{2,3},{3,2},{4,5},{5,4},{6,7},{7,6},{8,9},{9,8},{10,11... | collective-permute-start | bytes 196616 | tf_op jit(solution)/shard_map/ppermute | solution.py:251
  42.4 4.5 %collective-permute-start.12 = (bf16[128,256]{1,0:T(8,128)(2,1)S(1)}, bf16[128,256]{1,0:T(8,128)(2,1)S(1)}, u32[]{:S(2)}, u32[]{:S(2)}) collective-permute-start(bf16[128,256]{1,0:T(8,128)(2,1)S(1)} %get-tuple-element.37), channel_id=1, source_target_pairs={{0,2},{1,3},{2,0},{3,1},{4,6},{5,7},{6,4},{7,5},{8,10},{9,11},{10,... | collective-permute-start | bytes 196616 | tf_op jit(solution)/shard_map/ppermute | solution.py:251
  44.0 4.1 %collective-permute-start.13 = (bf16[128,256]{1,0:T(8,128)(2,1)S(1)}, bf16[128,256]{1,0:T(8,128)(2,1)S(1)}, u32[]{:S(2)}, u32[]{:S(2)}) collective-permute-start(bf16[128,256]{1,0:T(8,128)(2,1)S(1)} %get-tuple-element.38), channel_id=1, source_target_pairs={{0,3},{1,2},{2,1},{3,0},{4,7},{5,6},{6,5},{7,4},{8,11},{9,10},{10,... | collective-permute-start | bytes 196616 | tf_op jit(solution)/shard_map/ppermute | solution.py:251

commit v4 on v3

--- a/solution.py
+++ b/solution.py
@@ -196,20 +196,16 @@
         outs[j][...] = (sum_ref[span, :] * history ** (-0.5) + extra_ref[span, 0:width].astype(F32)).astype(BF16)
 
 
-def mix_kernel(users, ctx_size, head_size, held, *refs):
-    owner_ref, extra_ref, weight_ref = refs[:3]
-    sums = refs[3 : 3 + ctx_size]
-    packs = refs[3 + ctx_size : 2 + 2 * ctx_size]
-    outs = refs[2 + 2 * ctx_size : 2 + 2 * ctx_size + head_size]
-    residual_ref = refs[2 + 2 * ctx_size + head_size]
+def prepare_kernel(users, ctx_size, held, *refs):
+    owner_ref, extra_ref = refs[:2]
+    packs = refs[2:-2]
+    gate_ref, residual_ref = refs[-2:]
     me_user = lax.axis_index("users")
     me_ctx = lax.axis_index("ctx")
-    me_head = lax.axis_index("head")
     slots, width = residual_ref.shape
     owner = jnp.transpose(jnp.broadcast_to(owner_ref[...].astype(F32), (8, slots)))[:, 0:1]
-    lanes = 128
-    lane = lax.broadcasted_iota(jnp.int32, (slots, lanes), 1)
-    inside = jnp.zeros((slots, lanes), jnp.bool_)
+    lane = lax.broadcasted_iota(jnp.int32, (slots, 128), 1)
+    inside = jnp.zeros((slots, 128), jnp.bool_)
     for k in range(users):
         named = (me_user ^ k) * ctx_size + (me_ctx ^ lane)
         inside = inside | ((owner == named.astype(F32)) & (lane < ctx_size))
@@ -217,12 +213,9 @@
         lax.broadcasted_iota(jnp.int32, (slots, slots), 1) < lax.broadcasted_iota(jnp.int32, (slots, slots), 0)
     ).astype(F32).astype(BF16)
     rank = jnp.where(inside, dot(after, inside.astype(F32).astype(BF16)), -1.0)
-    attended = sums[0][...].astype(F32)
-    for m in range(1, ctx_size):
-        attended = attended + sums[m][...].astype(F32)
     both = extra_ref[0:slots, width:].astype(F32)
-    if ctx_size > 1:
-        spots = lax.broadcasted_iota(jnp.int32, (slots, (ctx_size - 1) * held), 1).astype(F32)
+    if packs:
+        spots = lax.broadcasted_iota(jnp.int32, (slots, len(packs) * held), 1).astype(F32)
         spot = jnp.full((slots, 1), -1.0, F32)
         for m in range(1, ctx_size):
             mine = rank[:, m : m + 1]
@@ -230,8 +223,19 @@
         both = both + dot(
             (spots == spot).astype(F32).astype(BF16), jnp.concatenate([pack[...] for pack in packs], axis=0)
         )
-    gates, residual = both[:, 0:width], both[:, width:]
-    residual_ref[...] = residual.astype(BF16)
+    gate_ref[...] = both[:, 0:width]
+    residual_ref[...] = both[:, width:].astype(BF16)
+
+
+def mix_kernel(ctx_size, *refs):
+    gate_ref, weight_ref = refs[:2]
+    sums = refs[2 : 2 + ctx_size]
+    outs = refs[2 + ctx_size :]
+    me_head = lax.axis_index("head")
+    width = gate_ref.shape[1]
+    attended = sums[0][...].astype(F32)
+    for one in sums[1:]:
+        attended = attended + one[...].astype(F32)
     parts = []
     for at in range(0, width, HEAD_DIM):
         one = attended[:, at : at + HEAD_DIM]
@@ -239,10 +243,10 @@
         parts.append(
             center
             * lax.rsqrt(jnp.mean(center * center, axis=1, keepdims=True) + 1e-05)
-            * gates[:, at : at + HEAD_DIM]
+            * gate_ref[:, at : at + HEAD_DIM]
         )
     hidden = jnp.concatenate(parts, axis=1).astype(BF16)
-    for t in range(head_size):
+    for t in range(len(outs)):
         first = pl.multiple_of((me_head ^ t) * width, width)
         outs[t][...] = dot(hidden, weight_ref[:, pl.ds(first, width)]).astype(outs[t].dtype)
 
@@ -296,10 +300,13 @@
         (pltpu.VMEM((count, width), F32),),
     )(spots, part, extra, key_cache[0], value_cache[0], *relays)
     sums = [sums[0]] + [swap(sums[m], "ctx", m) for m in range(1, ctx_size)]
-    *parts, residual = call(
-        lambda *refs: mix_kernel(users, ctx_size, head_size, held, *refs),
-        (shape((slots, width), F32),) + (shape((slots, width)),) * (head_size - 1) + (shape((slots, width)),),
-    )(owner, extra, out_weight, *sums, *packs)
+    gates, residual = call(
+        lambda *refs: prepare_kernel(users, ctx_size, held, *refs), (shape((slots, width), F32), shape((slots, width)))
+    )(owner, extra, *packs)
+    parts = call(
+        lambda *refs: mix_kernel(ctx_size, *refs),
+        (shape((slots, width), F32),) + (shape((slots, width)),) * (head_size - 1),
+    )(gates, out_weight, *sums)
     got = [parts[0]] + [swap(parts[t], "head", t) for t in range(1, head_size)]
     total = residual.astype(F32)
     for one in got:

time: 48.9 us -> 48.1 us (0.984)
  waiting for transfers between devices: 21.5 us -> 20.5 us
    ppermute x14, waiting for transfers between devices: 21.5 us -> 20.5 us  [swap(): lax.ppermute(x, axis, [(i, i ^ k) for i in range(lax.axis_size(axis))])]
    pallas_call x4 -> x5, Pallas kernels: 7.08 us -> 7.27 us  [run(): return made(*args)]
  transfers between devices with their start and end apart: 14 -> 14, of which waited for: 9 -> 8; matrix products, arithmetic and copies ran while one was open for 0% -> 0% of each run, Pallas kernels for 5% -> 7%
where the time goes in v4:
time: 48.1 us; the launch traced here: 47.9 us
  waiting for transfers between devices  20.5 us (43%)
  starting transfers between devices  18.6 us (39%)
  Pallas kernels  7.27 us (15%)
  between operations  0.77 us (2%)
  other arithmetic  0.74 us (2%)
    ppermute x14, waiting for transfers between devices, swap(): lax.ppermute(x, axis, [(i, i ^ k) for i in range(lax.axis_size(axis))])  20.5 us
    ppermute x14, starting transfers between devices, swap(): lax.ppermute(x, axis, [(i, i ^ k) for i in range(lax.axis_size(axis))])  18.6 us
    pallas_call x5, Pallas kernels, run(): return made(*args)  7.27 us
  transfers between devices with their start and end apart: 14, of which 8 were waited for; matrix products, arithmetic and copies ran while one was open for 0% of the time, Pallas kernels for 7%

profile of v4, /device:TPU:0, one launch (start us, length us, event | category | flops | bytes accessed | tf_op | source)
XLA Modules:
  0.0 47.9 jit_solution(17110884663218058690)
XLA Ops:
  0.0 0.0 copy-start.1
  0.0 0.0 copy-start.2
  0.0 3.7 %shard_map.82 = (bf16[144,256]{1,0:T(8,128)(2,1)S(1)}, bf16[128,768]{1,0:T(8,128)(2,1)S(1)}) custom-call(s32[1,128]{1,0:T(1,128)} %bitcast.9, s32[1,128]{1,0:T(1,128)} %row_ref.1, bf16[128,1024]{1,0:T(8,128)(2,1)} %table_hbm.1, bf16[1024,4,256]{2,1,0:T(4,128)(2,1)} %weight_hbm.1), custom_call_target="tpu_custom_call" | custom-call | tf_op jit(solution)/shard_map/pallas_call | solution.py:41
  3.8 0.0 copy-start.3
  3.8 3.1 %collective-permute-start = (bf16[144,256]{1,0:T(8,128)(2,1)S(1)}, bf16[144,256]{1,0:T(8,128)(2,1)S(1)}, u32[]{:S(2)}, u32[]{:S(2)}) collective-permute-start(bf16[144,256]{1,0:T(8,128)(2,1)S(1)} %get-tuple-element.23.refs_0_), channel_id=1, source_target_pairs={{0,4},{4,0},{8,12},{12,8},{1,5},{5,1},{9,13},{13,9},{2,6},{6,2},{1... | collective-permute-start | bytes 221192 | tf_op jit(solution)/shard_map/ppermute | solution.py:255
  6.9 2.6 %collective-permute-start.1 = (bf16[144,256]{1,0:T(8,128)(2,1)S(1)}, bf16[144,256]{1,0:T(8,128)(2,1)S(1)}, u32[]{:S(2)}, u32[]{:S(2)}) collective-permute-start(bf16[144,256]{1,0:T(8,128)(2,1)S(1)} %get-tuple-element.23.refs_0_), channel_id=1, source_target_pairs={{0,8},{4,12},{8,0},{12,4},{1,9},{5,13},{9,1},{13,5},{2,10},{6,14},... | collective-permute-start | bytes 221192 | tf_op jit(solution)/shard_map/ppermute | solution.py:255
  9.5 0.0 collective-permute-start.2
  9.5 0.0 collective-permute-done.refs_1_
  9.5 5.2 %collective-permute-done.1.refs_2_ = bf16[144,256]{1,0:T(8,128)(2,1)S(1)} collective-permute-done((bf16[144,256]{1,0:T(8,128)(2,1)S(1)}, bf16[144,256]{1,0:T(8,128)(2,1)S(1)}, u32[]{:S(2)}, u32[]{:S(2)}) %collective-permute-start.1) | collective-permute-done | bytes 73760 | tf_op jit(solution)/shard_map/ppermute | solution.py:255
  14.7 1.0 %collective-permute-done.2.refs_3_ = bf16[144,256]{1,0:T(8,128)(2,1)S(1)} collective-permute-done((bf16[144,256]{1,0:T(8,128)(2,1)S(1)}, bf16[144,256]{1,0:T(8,128)(2,1)S(1)}, u32[]{:S(2)}, u32[]{:S(2)}) %collective-permute-start.2) | collective-permute-done | bytes 73760 | tf_op jit(solution)/shard_map/ppermute | solution.py:255
  15.7 0.0 copy-start
  15.8 1.6 %collective-permute-start.7 = (bf16[512,256]{1,0:T(8,128)(2,1)S(1)}, bf16[512,256]{1,0:T(8,128)(2,1)S(1)}, u32[]{:S(2)}, u32[]{:S(2)}) collective-permute-start(bf16[512,256]{1,0:T(8,128)(2,1)S(1)} %pad_maximum_fusion.refs_4_), channel_id=1, source_target_pairs={{0,16},{16,0},{1,17},{17,1},{2,18},{18,2},{3,19},{19,3},{4,20},{20... | collective-permute-start | bytes 786440 | tf_op jit(solution)/shard_map/ppermute | solution.py:255
  17.3 0.5 %collective-permute-start.3 = (bf16[128,768]{1,0:T(8,128)(2,1)S(1)}, bf16[128,768]{1,0:T(8,128)(2,1)S(1)}, u32[]{:S(2)}, u32[]{:S(2)}) collective-permute-start(bf16[128,768]{1,0:T(8,128)(2,1)S(1)} %get-tuple-element.24.refs_5_), channel_id=1, source_target_pairs={{0,16},{16,0},{1,17},{17,1},{2,18},{18,2},{3,19},{19,3},{4,20},{20... | collective-permute-start | bytes 589832 | tf_op jit(solution)/shard_map/ppermute | solution.py:255
  17.9 8.4 %collective-permute-done.3.refs_6_ = bf16[128,768]{1,0:T(8,128)(2,1)S(1)} collective-permute-done((bf16[128,768]{1,0:T(8,128)(2,1)S(1)}, bf16[128,768]{1,0:T(8,128)(2,1)S(1)}, u32[]{:S(2)}, u32[]{:S(2)}) %collective-permute-start.3) | collective-permute-done | bytes 196640 | tf_op jit(solution)/shard_map/ppermute | solution.py:255
  26.3 1.5 %shard_map.83 = (bf16[64,512]{1,0:T(8,128)(2,1)S(1)}, bf16[64,512]{1,0:T(8,128)(2,1)S(1)}, bf16[64,512]{1,0:T(8,128)(2,1)S(1)}, bf16[512,768]{1,0:T(8,128)(2,1)S...) custom-call(bf16[144,256]{1,0:T(8,128)(2,1)S(1)} %get-tuple-element.23.refs_0_, ...), custom_call_target="tpu_custom_call" | custom-call | tf_op jit(solution)/shard_map/pallas_call | solution.py:41
  27.8 1.3 %collective-permute-start.4 = (bf16[64,512]{1,0:T(8,128)(2,1)S(1)}, bf16[64,512]{1,0:T(8,128)(2,1)S(1)}, u32[]{:S(2)}, u32[]{:S(2)}) collective-permute-start(bf16[64,512]{1,0:T(8,128)(2,1)S(1)} %get-tuple-element.26), channel_id=1, source_target_pairs={{0,4},{4,0},{8,12},{12,8},{1,5},{5,1},{9,13},{13,9},{2,6},{6,2},{1... | collective-permute-start | bytes 196616 | tf_op jit(solution)/shard_map/ppermute | solution.py:255
  29.1 1.6 %collective-permute-start.5 = (bf16[64,512]{1,0:T(8,128)(2,1)S(1)}, bf16[64,512]{1,0:T(8,128)(2,1)S(1)}, u32[]{:S(2)}, u32[]{:S(2)}) collective-permute-start(bf16[64,512]{1,0:T(8,128)(2,1)S(1)} %get-tuple-element.27), channel_id=1, source_target_pairs={{0,8},{4,12},{8,0},{12,4},{1,9},{5,13},{9,1},{13,5},{2,10},{6,14},... | collective-permute-start | bytes 196616 | tf_op jit(solution)/shard_map/ppermute | solution.py:255
  30.7 1.5 %collective-permute-start.6 = (bf16[64,512]{1,0:T(8,128)(2,1)S(1)}, bf16[64,512]{1,0:T(8,128)(2,1)S(1)}, u32[]{:S(2)}, u32[]{:S(2)}) collective-permute-start(bf16[64,512]{1,0:T(8,128)(2,1)S(1)} %get-tuple-element.28), channel_id=1, source_target_pairs={{0,12},{4,8},{8,4},{12,0},{1,13},{5,9},{9,5},{13,1},{2,14},{6,10},... | collective-permute-start | bytes 196616 | tf_op jit(solution)/shard_map/ppermute | solution.py:255
  32.2 0.0 collective-permute-done.7.refs_5_
  32.2 0.0 copy-done.1
  32.2 0.0 copy-done.2
  32.2 1.0 %shard_map.85 = (bf16[128,256]{1,0:T(8,128)(2,1)S(1)}, bf16[128,256]{1,0:T(8,128)(2,1)S(1)}, bf16[128,256]{1,0:T(8,128)(2,1)S(1)}, bf16[128,256]{1,0:T(8,128)(2,1)S(1)}) custom-call(f32[512,128]{1,0:T(8,128)S(1)} %get-tuple-element.31.refs_0_, bf16[512,256]{1,0:T(8,128)(2,1)S(1)} %get-tuple-element.32.refs_1_, ...), custom_call_target="tpu_custom_call" | custom-call | tf_op jit(solution)/shard_map/pallas_call | solution.py:41
  33.2 2.4 %collective-permute-start.10 = (bf16[128,256]{1,0:T(8,128)(2,1)S(1)}, bf16[128,256]{1,0:T(8,128)(2,1)S(1)}, u32[]{:S(2)}, u32[]{:S(2)}) collective-permute-start(bf16[128,256]{1,0:T(8,128)(2,1)S(1)} %get-tuple-element.36), channel_id=1, source_target_pairs={{0,12},{4,8},{8,4},{12,0},{1,13},{5,9},{9,5},{13,1},{2,14},{6,10},... | collective-permute-start | bytes 196616 | tf_op jit(solution)/shard_map/ppermute | solution.py:255
  35.6 0.2 collective-permute-start.8
  35.8 0.0 collective-permute-done.4.refs_2_
  35.8 1.9 %collective-permute-start.9 = (bf16[128,256]{1,0:T(8,128)(2,1)S(1)}, bf16[128,256]{1,0:T(8,128)(2,1)S(1)}, u32[]{:S(2)}, u32[]{:S(2)}) collective-permute-start(bf16[128,256]{1,0:T(8,128)(2,1)S(1)} %get-tuple-element.35), channel_id=1, source_target_pairs={{0,8},{4,12},{8,0},{12,4},{1,9},{5,13},{9,1},{13,5},{2,10},{6,14},... | collective-permute-start | bytes 196616 | tf_op jit(solution)/shard_map/ppermute | solution.py:255
  38.4 0.0 collective-permute-done.5.refs_3_
  38.4 0.0 collective-permute-done.6.refs_4_
  38.4 0.0 copy-done.3
  38.4 0.7 %shard_map.84 = (f32[128,256]{1,0:T(8,128)S(1)}, bf16[128,256]{1,0:T(8,128)(2,1)S(1)}) custom-call(s32[1,128]{1,0:T(1,128)S(1)} %bitcast.10, bf16[512,768]{1,0:T(8,128)(2,1)S(1)} %get-tuple-element.25.refs_1_.refs_2_, bf16[64,512]{1,0:T(8,128)(2,1)S(1)} %collective-permute-done.4.refs_2_, bf16[64,512]{1,0:T(8,128)(2,1)S(1)} %collective-permute-done.5.refs_3_, ...), custom_call_target="tpu_custom_call" | custom-call | tf_op jit(solution)/shard_map/pallas_call | solution.py:41
  39.1 0.5 collective-permute-done.10.refs_5_
  39.5 0.7 %collective-permute-done.8.refs_3_ = bf16[128,256]{1,0:T(8,128)(2,1)S(1)} collective-permute-done((bf16[128,256]{1,0:T(8,128)(2,1)S(1)}, bf16[128,256]{1,0:T(8,128)(2,1)S(1)}, u32[]{:S(2)}, u32[]{:S(2)}) %collective-permute-start.8) | collective-permute-done | bytes 65568 | tf_op jit(solution)/shard_map/ppermute | solution.py:255
  40.2 0.8 %collective-permute-done.9.refs_4_ = bf16[128,256]{1,0:T(8,128)(2,1)S(1)} collective-permute-done((bf16[128,256]{1,0:T(8,128)(2,1)S(1)}, bf16[128,256]{1,0:T(8,128)(2,1)S(1)}, u32[]{:S(2)}, u32[]{:S(2)}) %collective-permute-start.9) | collective-permute-done | bytes 65568 | tf_op jit(solution)/shard_map/ppermute | solution.py:255
  41.1 0.0 copy-done
  41.1 0.4 shard_map.86
  41.5 0.1 collective-permute-start.11
  41.5 1.6 %collective-permute-start.12 = (bf16[128,256]{1,0:T(8,128)(2,1)S(1)}, bf16[128,256]{1,0:T(8,128)(2,1)S(1)}, u32[]{:S(2)}, u32[]{:S(2)}) collective-permute-start(bf16[128,256]{1,0:T(8,128)(2,1)S(1)} %get-tuple-element.39), channel_id=1, source_target_pairs={{0,2},{1,3},{2,0},{3,1},{4,6},{5,7},{6,4},{7,5},{8,10},{9,11},{10,... | collective-permute-start | bytes 196616 | tf_op jit(solution)/shard_map/ppermute | solution.py:255
  43.1 0.3 collective-permute-start.13
  43.4 0.0 collective-permute-done.11
  43.4 2.6 %collective-permute-done.12 = bf16[128,256]{1,0:T(8,128)(2,1)S(1)} collective-permute-done((bf16[128,256]{1,0:T(8,128)(2,1)S(1)}, bf16[128,256]{1,0:T(8,128)(2,1)S(1)}, u32[]{:S(2)}, u32[]{:S(2)}) %collective-permute-start.12) | collective-permute-done | bytes 65568 | tf_op jit(solution)/shard_map/ppermute | solution.py:255
  46.0 1.1 %collective-permute-done.13 = bf16[128,256]{1,0:T(8,128)(2,1)S(1)} collective-permute-done((bf16[128,256]{1,0:T(8,128)(2,1)S(1)}, bf16[128,256]{1,0:T(8,128)(2,1)S(1)}, u32[]{:S(2)}, u32[]{:S(2)}) %collective-permute-start.13) | collective-permute-done | bytes 65568 | tf_op jit(solution)/shard_map/ppermute | solution.py:255
  47.2 0.7 %fusion = bf16[1,128,256]{2,1,0:T(8,128)(2,1)} fusion(bf16[128,256]{1,0:T(8,128)(2,1)S(1)} %collective-permute-done.13, bf16[128,256]{1,0:T(8,128)(2,1)S(1)} %collective-permute-done.12, bf16[128,256]{1,0:T(8,128)(2,1)S(1)} %collective-permute-done.11, f32[128,256]{1,0:T(8,128)S(1)} %get-tuple-element.37, bf16[128,256]{1,0:T(8,128)(2,1)S(1)} %get-tuple-element.29, ...), kind=kLoop, calls=%fused_computation.2 | loop fusion | flops 327680 | bytes 458880 | tf_op jit(solution)/shard_map/broadcast_in_dim | solution.py:315
  (6 shorter events, 0.0 us)
Async XLA Ops:
  0.0 32.2 %copy-start.1 = (bf16[1,512,256]{2,1,0:T(8,128)(2,1)S(1)}, bf16[1,512,256]{2,1,0:T(8,128)(2,1)}, u32[]{:S(2)}) copy-start(bf16[1,512,256]{2,1,0:T(8,128)(2,1)} %param.14) | copy-start | bytes 786436
  0.0 32.2 %copy-start.2 = (bf16[1,512,256]{2,1,0:T(8,128)(2,1)S(1)}, bf16[1,512,256]{2,1,0:T(8,128)(2,1)}, u32[]{:S(2)}) copy-start(bf16[1,512,256]{2,1,0:T(8,128)(2,1)} %param.15) | copy-start | bytes 786436
  3.8 34.6 %copy-start.3 = (s32[1,128,1]{1,2,0:T(1,128)S(1)}, s32[1,128,1]{1,2,0:T(1,128)}, u32[]{:S(2)}) copy-start(s32[1,128,1]{1,2,0:T(1,128)} %param.9) | copy-start | bytes 1540
  3.8 5.7 %collective-permute-start = (bf16[144,256]{1,0:T(8,128)(2,1)S(1)}, bf16[144,256]{1,0:T(8,128)(2,1)S(1)}, u32[]{:S(2)}, u32[]{:S(2)}) collective-permute-start(bf16[144,256]{1,0:T(8,128)(2,1)S(1)} %get-tuple-element.23.refs_0_), channel_id=1, source_target_pairs={{0,4},{4,0},{8,12},{12,8},{1,5},{5,1},{9,13},{13,9},{2,6},{6,2},{1... | collective-permute-start | bytes 221192 | tf_op jit(solution)/shard_map/ppermute | solution.py:255
  6.9 7.8 %collective-permute-start.1 = (bf16[144,256]{1,0:T(8,128)(2,1)S(1)}, bf16[144,256]{1,0:T(8,128)(2,1)S(1)}, u32[]{:S(2)}, u32[]{:S(2)}) collective-permute-start(bf16[144,256]{1,0:T(8,128)(2,1)S(1)} %get-tuple-element.23.refs_0_), channel_id=1, source_target_pairs={{0,8},{4,12},{8,0},{12,4},{1,9},{5,13},{9,1},{13,5},{2,10},{6,14},... | collective-permute-start | bytes 221192 | tf_op jit(solution)/shard_map/ppermute | solution.py:255
  9.5 6.3 %collective-permute-start.2 = (bf16[144,256]{1,0:T(8,128)(2,1)S(1)}, bf16[144,256]{1,0:T(8,128)(2,1)S(1)}, u32[]{:S(2)}, u32[]{:S(2)}) collective-permute-start(bf16[144,256]{1,0:T(8,128)(2,1)S(1)} %get-tuple-element.23.refs_0_), channel_id=1, source_target_pairs={{0,12},{4,8},{8,4},{12,0},{1,13},{5,9},{9,5},{13,1},{2,14},{6,10},... | collective-permute-start | bytes 221192 | tf_op jit(solution)/shard_map/ppermute | solution.py:255
  15.7 25.3 %copy-start = (bf16[256,1024]{1,0:T(8,128)(2,1)S(1)}, bf16[256,1024]{1,0:T(8,128)(2,1)}, u32[]{:S(2)}) copy-start(bf16[256,1024]{1,0:T(8,128)(2,1)} %refs_1_.1) | copy-start | bytes 1572868
  15.8 16.5 %collective-permute-start.7 = (bf16[512,256]{1,0:T(8,128)(2,1)S(1)}, bf16[512,256]{1,0:T(8,128)(2,1)S(1)}, u32[]{:S(2)}, u32[]{:S(2)}) collective-permute-start(bf16[512,256]{1,0:T(8,128)(2,1)S(1)} %pad_maximum_fusion.refs_4_), channel_id=1, source_target_pairs={{0,16},{16,0},{1,17},{17,1},{2,18},{18,2},{3,19},{19,3},{4,20},{20... | collective-permute-start | bytes 786440 | tf_op jit(solution)/shard_map/ppermute | solution.py:255
  17.3 9.0 %collective-permute-start.3 = (bf16[128,768]{1,0:T(8,128)(2,1)S(1)}, bf16[128,768]{1,0:T(8,128)(2,1)S(1)}, u32[]{:S(2)}, u32[]{:S(2)}) collective-permute-start(bf16[128,768]{1,0:T(8,128)(2,1)S(1)} %get-tuple-element.24.refs_5_), channel_id=1, source_target_pairs={{0,16},{16,0},{1,17},{17,1},{2,18},{18,2},{3,19},{19,3},{4,20},{20... | collective-permute-start | bytes 589832 | tf_op jit(solution)/shard_map/ppermute | solution.py:255
  27.8 8.0 %collective-permute-start.4 = (bf16[64,512]{1,0:T(8,128)(2,1)S(1)}, bf16[64,512]{1,0:T(8,128)(2,1)S(1)}, u32[]{:S(2)}, u32[]{:S(2)}) collective-permute-start(bf16[64,512]{1,0:T(8,128)(2,1)S(1)} %get-tuple-element.26), channel_id=1, source_target_pairs={{0,4},{4,0},{8,12},{12,8},{1,5},{5,1},{9,13},{13,9},{2,6},{6,2},{1... | collective-permute-start | bytes 196616 | tf_op jit(solution)/shard_map/ppermute | solution.py:255
  29.1 9.3 %collective-permute-start.5 = (bf16[64,512]{1,0:T(8,128)(2,1)S(1)}, bf16[64,512]{1,0:T(8,128)(2,1)S(1)}, u32[]{:S(2)}, u32[]{:S(2)}) collective-permute-start(bf16[64,512]{1,0:T(8,128)(2,1)S(1)} %get-tuple-element.27), channel_id=1, source_target_pairs={{0,8},{4,12},{8,0},{12,4},{1,9},{5,13},{9,1},{13,5},{2,10},{6,14},... | collective-permute-start | bytes 196616 | tf_op jit(solution)/shard_map/ppermute | solution.py:255
  30.7 7.7 %collective-permute-start.6 = (bf16[64,512]{1,0:T(8,128)(2,1)S(1)}, bf16[64,512]{1,0:T(8,128)(2,1)S(1)}, u32[]{:S(2)}, u32[]{:S(2)}) collective-permute-start(bf16[64,512]{1,0:T(8,128)(2,1)S(1)} %get-tuple-element.28), channel_id=1, source_target_pairs={{0,12},{4,8},{8,4},{12,0},{1,13},{5,9},{9,5},{13,1},{2,14},{6,10},... | collective-permute-start | bytes 196616 | tf_op jit(solution)/shard_map/ppermute | solution.py:255
  33.2 6.3 %collective-permute-start.10 = (bf16[128,256]{1,0:T(8,128)(2,1)S(1)}, bf16[128,256]{1,0:T(8,128)(2,1)S(1)}, u32[]{:S(2)}, u32[]{:S(2)}) collective-permute-start(bf16[128,256]{1,0:T(8,128)(2,1)S(1)} %get-tuple-element.36), channel_id=1, source_target_pairs={{0,12},{4,8},{8,4},{12,0},{1,13},{5,9},{9,5},{13,1},{2,14},{6,10},... | collective-permute-start | bytes 196616 | tf_op jit(solution)/shard_map/ppermute | solution.py:255
  35.6 4.6 %collective-permute-start.8 = (bf16[128,256]{1,0:T(8,128)(2,1)S(1)}, bf16[128,256]{1,0:T(8,128)(2,1)S(1)}, u32[]{:S(2)}, u32[]{:S(2)}) collective-permute-start(bf16[128,256]{1,0:T(8,128)(2,1)S(1)} %get-tuple-element.34), channel_id=1, source_target_pairs={{0,4},{4,0},{8,12},{12,8},{1,5},{5,1},{9,13},{13,9},{2,6},{6,2},{1... | collective-permute-start | bytes 196616 | tf_op jit(solution)/shard_map/ppermute | solution.py:255
  35.8 5.3 %collective-permute-start.9 = (bf16[128,256]{1,0:T(8,128)(2,1)S(1)}, bf16[128,256]{1,0:T(8,128)(2,1)S(1)}, u32[]{:S(2)}, u32[]{:S(2)}) collective-permute-start(bf16[128,256]{1,0:T(8,128)(2,1)S(1)} %get-tuple-element.35), channel_id=1, source_target_pairs={{0,8},{4,12},{8,0},{12,4},{1,9},{5,13},{9,1},{13,5},{2,10},{6,14},... | collective-permute-start | bytes 196616 | tf_op jit(solution)/shard_map/ppermute | solution.py:255
  41.5 1.9 %collective-permute-start.11 = (bf16[128,256]{1,0:T(8,128)(2,1)S(1)}, bf16[128,256]{1,0:T(8,128)(2,1)S(1)}, u32[]{:S(2)}, u32[]{:S(2)}) collective-permute-start(bf16[128,256]{1,0:T(8,128)(2,1)S(1)} %get-tuple-element.38), channel_id=1, source_target_pairs={{0,1},{1,0},{2,3},{3,2},{4,5},{5,4},{6,7},{7,6},{8,9},{9,8},{10,11... | collective-permute-start | bytes 196616 | tf_op jit(solution)/shard_map/ppermute | solution.py:255
  41.5 4.5 %collective-permute-start.12 = (bf16[128,256]{1,0:T(8,128)(2,1)S(1)}, bf16[128,256]{1,0:T(8,128)(2,1)S(1)}, u32[]{:S(2)}, u32[]{:S(2)}) collective-permute-start(bf16[128,256]{1,0:T(8,128)(2,1)S(1)} %get-tuple-element.39), channel_id=1, source_target_pairs={{0,2},{1,3},{2,0},{3,1},{4,6},{5,7},{6,4},{7,5},{8,10},{9,11},{10,... | collective-permute-start | bytes 196616 | tf_op jit(solution)/shard_map/ppermute | solution.py:255
  43.1 4.1 %collective-permute-start.13 = (bf16[128,256]{1,0:T(8,128)(2,1)S(1)}, bf16[128,256]{1,0:T(8,128)(2,1)S(1)}, u32[]{:S(2)}, u32[]{:S(2)}) collective-permute-start(bf16[128,256]{1,0:T(8,128)(2,1)S(1)} %get-tuple-element.40), channel_id=1, source_target_pairs={{0,3},{1,2},{2,1},{3,0},{4,7},{5,6},{6,5},{7,4},{8,11},{9,10},{10,... | collective-permute-start | bytes 196616 | tf_op jit(solution)/shard_map/ppermute | solution.py:255
